TPU v7x, 128 devices: a whole 4x4x4 slice. The times are simulated.
128 devices in a mesh: theta: 16 (over z, x_hi, core), gz: 8 (over x_lo, y).
Axes of the slice: x: 4 (x_hi: 2, x_lo: 2; x = x_hi * 2 + x_lo), y: 4, z: 4, core: 2. Of those that a mesh axis runs over, the one named last changes fastest.
Arguments:
- velocity: float32 [3, 512, 256, 128], P(None, 'theta', 'gz'), may hold values from -3 to 3
Outputs:
- viscosity_ratio: float32 [512, 256, 128], P('theta', 'gz')
- pressure_modes: float32 [2, 512, 256, 128], P(None, 'gz', 'theta')
All inputs are finite; a program needn't handle non-finite values.
Results may differ from a plain program's by a relative error of at most 0.0003.
Values sent between devices are 32-bit elements; how exact they have to be, the bound alone decides.
A program may use at most 128 MiB of HBM per device.

v0:
```python
import functools
import math

import jax
import jax.numpy as jnp
import ml_dtypes
import numpy as np
from jax import lax
from jax.experimental import pallas as pl
from jax.experimental.pallas import tpu as pltpu
from jax.sharding import PartitionSpec as P

NTH = 512
NZ = 256
NR = 128


pipe_length = 4.0 * math.pi
nu_molecular = 5e-05
time_step = 2.0
filter_ratio = 4.0
epsilon_den = 1e-06
pair_first = (0, 1, 2, 0, 0, 1)
pair_second = (0, 1, 2, 1, 2, 2)


def with_halo(block, sides, width):
    for axis, dim in sides:
        count = lax.axis_size(axis)
        forward = [(i, i + 1) for i in range(count - 1)]
        forward.append((count - 1, 0))
        backward = [(target, source) for source, target in forward]
        low = lax.ppermute(
            lax.slice_in_dim(block, block.shape[dim] - width, None, axis=dim), axis, forward
        )
        high = lax.ppermute(lax.slice_in_dim(block, 0, width, axis=dim), axis, backward)
        block = jnp.concatenate([low, block, high], axis=dim)
    return block


def grid_terms():
    radial_step = 1.0 / NR
    radius = (jnp.arange(NR, dtype=jnp.float32) + 0.5) * radial_step
    theta_step = 2.0 * math.pi / NTH
    axial_step = pipe_length / NZ
    width_sq = jnp.cbrt(radial_step * radius * theta_step * axial_step) ** 2
    return (radius, width_sq)


def along_theta(padded):
    return (padded[..., 2:, 1:-1, :] - padded[..., :-2, 1:-1, :]) * (0.5 * NTH / (2.0 * math.pi))


def along_axis(padded):
    return (padded[..., 1:-1, 2:, :] - padded[..., 1:-1, :-2, :]) * (0.5 * NZ / pipe_length)


def along_radius(field):
    zeros = jnp.zeros(field.shape[:-1] + (1,), field.dtype)
    extended = jnp.concatenate([zeros, field, zeros], axis=-1)
    return (extended[..., 2:] - extended[..., :-2]) * (0.5 * NR)


def interior(padded):
    return padded[..., 1:-1, 1:-1, :]


def strain(padded, radius):
    centre = interior(padded)
    radial = along_radius(centre)
    azimuthal = along_theta(padded) / radius
    axial = along_axis(padded)
    return jnp.stack(
        [
            radial[0],
            azimuthal[1] + centre[0] / radius,
            axial[2],
            0.5 * (radial[1] - centre[1] / radius + azimuthal[0]),
            0.5 * (axial[0] + radial[2]),
            0.5 * (azimuthal[2] + axial[1]),
        ]
    )


def magnitude(tensor):
    return jnp.sqrt(
        2.0 * (tensor[0] ** 2 + tensor[1] ** 2 + tensor[2] ** 2)
        + 4.0 * (tensor[3] ** 2 + tensor[4] ** 2 + tensor[5] ** 2)
    )


def test_filter(padded):
    across = (
        0.25 * padded[..., :-2, :, :] + 0.5 * padded[..., 1:-1, :, :] + 0.25 * padded[..., 2:, :, :]
    )
    return (
        0.25 * across[..., :, :-2, :] + 0.5 * across[..., :, 1:-1, :] + 0.25 * across[..., :, 2:, :]
    )


def products(flow, tensor):
    pairs = jnp.stack(
        [
            flow[first_comp] * flow[second_comp]
            for first_comp, second_comp in zip(pair_first, pair_second)
        ]
    )
    return jnp.concatenate([flow, pairs, tensor, magnitude(tensor) * tensor], axis=0)


def germano(filtered, width_sq):
    means = filtered[0:3]
    pairs = jnp.stack(
        [
            means[first_comp] * means[second_comp]
            for first_comp, second_comp in zip(pair_first, pair_second)
        ]
    )
    leonard = filtered[3:9] - pairs
    smooth = filtered[9:15]
    model = 2.0 * width_sq * (filter_ratio * magnitude(smooth) * smooth - filtered[15:21])
    weights = jnp.array([1.0, 1.0, 1.0, 2.0, 2.0, 2.0], dtype=jnp.float32)[:, None, None, None]
    return (
        jnp.sum(weights * leonard * model, axis=(0, 1, 2)),
        jnp.sum(weights * model * model, axis=(0, 1, 2)),
    )


def divergence(stress, radius):
    centre = interior(stress)
    radial = along_radius(centre)
    azimuthal = along_theta(stress) / radius
    axial = along_axis(stress)
    return jnp.stack(
        [
            radial[0] + azimuthal[3] + axial[4] + (centre[0] - centre[1]) / radius,
            radial[3] + azimuthal[1] + axial[5] + 2.0 * centre[3] / radius,
            radial[4] + azimuthal[5] + axial[2] + centre[4] / radius,
        ]
    )


def continuity(padded, radius):
    centre = interior(padded)
    return (
        along_radius(radius * centre[0]) / radius
        + along_theta(padded[1]) / radius
        + along_axis(padded[2])
    )


THETA_COUNT = 16
GZ_COUNT = 8
DEVICES = THETA_COUNT * GZ_COUNT
LOCAL_T = NTH // THETA_COUNT
LOCAL_Z = NZ // GZ_COUNT
LOCAL_M = NTH // GZ_COUNT
LOCAL_K = NZ // THETA_COUNT
MESH_ID = pl.DeviceIdType.MESH
HALF = NR // 2


def split_table(table):
    parts, rest = [], table
    for _ in range(3):
        part = rest.astype(np.float32).astype(ml_dtypes.bfloat16)
        parts.append(part)
        rest = rest - part.astype(np.float64)
    return np.stack(parts)


def axial_table():
    order = np.arange(NZ)
    block, rest = order // LOCAL_Z, order % LOCAL_Z
    cells = block * LOCAL_Z + 4 * (rest % 8) + rest // 8
    angle = 2.0 * np.pi * ((np.arange(NZ)[:, None] * cells[None, :]) % NZ) / NZ
    return split_table(np.concatenate([np.cos(angle), np.sin(angle)], axis=0))


def cycle_table():
    angle = 2.0 * np.pi * ((np.arange(NTH)[:, None] * np.arange(NTH)[None, :]) % NTH) / NTH
    scale = 1.0 / math.sqrt(NTH * NZ)
    cosine = (np.cos(angle) * scale).reshape(NTH, GZ_COUNT, LOCAL_M)
    sine = (np.sin(angle) * scale).reshape(NTH, GZ_COUNT, LOCAL_M)
    upper = np.stack([cosine, -sine], axis=2)
    lower = np.stack([-sine, -cosine], axis=2)
    both = np.concatenate([upper, lower], axis=0).reshape(2 * NTH, GZ_COUNT // 2, 4 * LOCAL_M)
    return split_table(np.moveaxis(both, 1, 0))


def split_value(value):
    parts = []
    for _ in range(3):
        part = value.astype(jnp.bfloat16)
        parts.append(part)
        value = value - part.astype(jnp.float32)
    return parts


def product(left, right):
    total = None
    for i, j in ((0, 2), (2, 0), (1, 1), (0, 1), (1, 0), (0, 0)):
        term = jnp.dot(left[i], right[j], preferred_element_type=jnp.float32)
        total = term if total is None else total + term
    return total


def wait_bytes(ref, sem):
    pltpu.make_async_copy(ref, ref, sem).wait()


def meet_all(row, column, barrier, second):
    def greet_row(i, carry):
        pl.semaphore_signal(
            barrier,
            inc=1,
            device_id={"theta": lax.rem(row + i, THETA_COUNT), "gz": column},
            device_id_type=MESH_ID,
        )
        return carry

    def greet_column(sem):
        def greet(i, carry):
            pl.semaphore_signal(
                sem,
                inc=1,
                device_id={"theta": row, "gz": lax.rem(column + i, GZ_COUNT)},
                device_id_type=MESH_ID,
            )
            return carry

        return greet

    lax.fori_loop(1, THETA_COUNT, greet_row, 0)
    lax.fori_loop(1, GZ_COUNT, greet_column(barrier), 0)
    pl.semaphore_wait(barrier, THETA_COUNT + GZ_COUNT - 2)
    lax.fori_loop(1, GZ_COUNT, greet_column(second), 0)
    pl.semaphore_wait(second, GZ_COUNT - 1)


def spectral_kernel(
    tiles_ref,
    axial_hbm,
    cycle_hbm,
    modes_ref,
    planes,
    plane,
    axial,
    cycle,
    left,
    spectrum,
    second,
    table_sem,
    send_sem,
    recv_sem,
    out_send_sem,
    out_recv_sem,
    own_sem,
):
    row, column = lax.axis_index("theta"), lax.axis_index("gz")
    me = row * GZ_COUNT + column
    fetch_axial = pltpu.make_async_copy(axial_hbm, axial, table_sem.at[0])
    fetch_cycle = pltpu.make_async_copy(cycle_hbm, cycle, table_sem.at[1])
    fetch_axial.start()
    fetch_cycle.start()
    meet_all(row, column, pltpu.get_barrier_semaphore(), second)

    def send_tile(i, carry):
        target = lax.rem(me + i, DEVICES)
        pltpu.make_async_remote_copy(
            src_ref=tiles_ref.at[target],
            dst_ref=planes.at[me],
            send_sem=send_sem,
            recv_sem=recv_sem,
            device_id={"theta": target // GZ_COUNT, "gz": lax.rem(target, GZ_COUNT)},
            device_id_type=MESH_ID,
        ).start()
        return carry

    lax.fori_loop(1, DEVICES, send_tile, 0)
    planes[me] = tiles_ref[me]
    wait_bytes(planes.at[pl.ds(0, DEVICES - 1)], recv_sem)
    wait_bytes(planes.at[pl.ds(0, DEVICES - 1)], send_sem)

    group = lax.broadcasted_iota(jnp.int32, (8, 128), 1) // LOCAL_T

    def gather_lines(c, carry):
        for quad in range(THETA_COUNT // 4):
            parts = [planes[(4 * quad + b) * GZ_COUNT + c] for b in range(4)]
            for z in range(4):
                turned = [
                    parts[b] if b == z else pltpu.roll(parts[b], ((b - z) * LOCAL_T) % 128, 1)
                    for b in range(4)
                ]
                value = jnp.where(
                    group < 2,
                    jnp.where(group == 0, turned[0], turned[1]),
                    jnp.where(group == 2, turned[2], turned[3]),
                )
                start = pl.multiple_of(c * LOCAL_Z + 8 * z, 8)
                plane[pl.ds(start, 8), 128 * quad : 128 * quad + 128] = value
        return carry

    lax.fori_loop(0, GZ_COUNT, gather_lines, 0)
    fetch_axial.wait()
    lines = product(axial, split_value(plane[...]))
    for n, part in enumerate(split_value(lines)):
        left[n, :, :NTH] = part[:NZ]
        left[n, :, NTH:] = part[NZ:]
    fetch_cycle.wait()

    def transform(step, carry):
        pair = lax.rem(column // 2 + step, GZ_COUNT // 2)
        both = product(left, cycle.at[:, pair])
        spectrum[2 * pair] = both[:, :128]
        spectrum[2 * pair + 1] = both[:, 128:]

        def send_modes(i, inner):
            target_column = 2 * pair + lax.rem(column + i // THETA_COUNT, 2)
            target_row = lax.rem(row + i, THETA_COUNT)
            rows = pl.ds(pl.multiple_of(target_row * LOCAL_K, LOCAL_K), LOCAL_K)

            @pl.when(jnp.logical_or(target_row != row, target_column != column))
            def _():
                pltpu.make_async_remote_copy(
                    src_ref=spectrum.at[target_column, rows],
                    dst_ref=modes_ref.at[me],
                    send_sem=out_send_sem,
                    recv_sem=out_recv_sem,
                    device_id={"theta": target_row, "gz": target_column},
                    device_id_type=MESH_ID,
                ).start()

            return inner

        lax.fori_loop(0, 2 * THETA_COUNT, send_modes, 0)
        return carry

    lax.fori_loop(0, GZ_COUNT // 2, transform, 0)
    own_rows = pl.ds(pl.multiple_of(row * LOCAL_K, LOCAL_K), LOCAL_K)
    keep = pltpu.make_async_copy(spectrum.at[column, own_rows], modes_ref.at[me], own_sem)
    keep.start()
    keep.wait()
    wait_bytes(modes_ref.at[pl.ds(0, DEVICES - 1)], out_send_sem)
    wait_bytes(modes_ref.at[pl.ds(0, DEVICES - 1)], out_recv_sem)


def spectral(tiles):
    any_space = pl.BlockSpec(memory_space=pl.ANY)
    return pl.pallas_call(
        spectral_kernel,
        out_shape=jax.ShapeDtypeStruct((DEVICES, LOCAL_K, 128), jnp.float32),
        in_specs=[pl.BlockSpec(memory_space=pltpu.VMEM), any_space, any_space],
        out_specs=any_space,
        scratch_shapes=[
            pltpu.VMEM((DEVICES, 8, 128), jnp.float32),
            pltpu.VMEM((NZ, NTH), jnp.float32),
            pltpu.VMEM((3, 2 * NZ, NZ), jnp.bfloat16),
            pltpu.VMEM((3, GZ_COUNT // 2, 2 * NTH, 4 * LOCAL_M), jnp.bfloat16),
            pltpu.VMEM((3, NZ, 2 * NTH), jnp.bfloat16),
            pltpu.VMEM((GZ_COUNT, NZ, 128), jnp.float32),
            pltpu.SemaphoreType.REGULAR,
            pltpu.SemaphoreType.DMA((2,)),
            pltpu.SemaphoreType.DMA,
            pltpu.SemaphoreType.DMA,
            pltpu.SemaphoreType.DMA,
            pltpu.SemaphoreType.DMA,
            pltpu.SemaphoreType.DMA,
        ],
        compiler_params=pltpu.CompilerParams(
            collective_id=0, has_side_effects=True, vmem_limit_bytes=48 << 20
        ),
        name="spectral",
    )(tiles, jnp.asarray(axial_table()), jnp.asarray(cycle_table()))


def solve_kernel(modes_ref, out_ref, inverse, partial, pressure):
    row, column = lax.axis_index("theta"), lax.axis_index("gz")
    shape = (LOCAL_K, 128)
    theta_mode = column * LOCAL_M + lax.broadcasted_iota(jnp.int32, shape, 1) % LOCAL_M
    axial_mode = row * LOCAL_K + lax.broadcasted_iota(jnp.int32, shape, 0)
    theta_wave = jnp.minimum(theta_mode, NTH - theta_mode).astype(jnp.float32)
    axial_wave = jnp.minimum(axial_mode, NZ - axial_mode).astype(jnp.float32) * (
        2.0 * math.pi / pipe_length
    )
    theta_sq = theta_wave * theta_wave
    axial_sq = axial_wave * axial_wave * (1.0 / (NR * NR))

    def diagonal(i):
        middle = i + 0.5
        extra = float(NR) if i == NR - 1 else 0.0
        return theta_sq * (1.0 / middle) + (axial_sq * middle + (2.0 * i + 1.0 + extra))

    def load(i):
        return modes_ref[i] * (-(i + 0.5) / (NR * NR))

    low_diag, low_value = diagonal(0), load(0)
    high_diag, high_value = diagonal(NR - 1), load(NR - 1)
    for step in range(1, HALF):
        i = step
        low_inverse = 1.0 / low_diag
        inverse[i - 1] = low_inverse
        partial[i - 1] = low_value
        low_value = load(i) + (low_inverse * float(i)) * low_value
        low_diag = diagonal(i) - low_inverse * float(i * i)
        j = NR - 1 - step
        high_inverse = 1.0 / high_diag
        inverse[j + 1] = high_inverse
        partial[j + 1] = high_value
        high_value = load(j) + (high_inverse * float(j + 1)) * high_value
        high_diag = diagonal(j) - high_inverse * float((j + 1) * (j + 1))
    scale = 1.0 / (low_diag * high_diag - float(HALF * HALF))
    low = (low_value * high_diag + float(HALF) * high_value) * scale
    high = (high_value * low_diag + float(HALF) * low_value) * scale
    pressure[HALF - 1] = low
    pressure[HALF] = high
    for step in range(1, HALF):
        i = HALF - 1 - step
        low = (partial[i] + float(i + 1) * low) * inverse[i]
        pressure[i] = low
        j = HALF + step
        high = (partial[j] + float(j) * high) * inverse[j]
        pressure[j] = high
    for k in range(LOCAL_K):
        out_ref[:, k, :] = pressure[:, k, :].T


def solve(modes):
    vmem = pl.BlockSpec(memory_space=pltpu.VMEM)
    out = pl.pallas_call(
        solve_kernel,
        out_shape=jax.ShapeDtypeStruct((2 * LOCAL_M, LOCAL_K, NR), jnp.float32),
        in_specs=[vmem],
        out_specs=vmem,
        scratch_shapes=[pltpu.VMEM((NR, LOCAL_K, 128), jnp.float32)] * 3,
        compiler_params=pltpu.CompilerParams(vmem_limit_bytes=32 << 20),
        name="solve",
    )(modes)
    return out.reshape(2, LOCAL_M, LOCAL_K, NR)


def body(velocity):
    radius, width_sq = grid_terms()
    wide_faces = None
    wide_faces = with_halo(velocity, (("theta", 1), ("gz", 2)), 3)
    tensor_wide = strain(wide_faces, radius)
    tensor_cycle = interior(tensor_wide)
    filtered = test_filter(products(interior(interior(wide_faces)), tensor_cycle))
    tensor = interior(tensor_cycle)
    numer, denom = germano(filtered, width_sq)
    numer, denom = lax.psum((numer, denom), ("theta", "gz"))
    coefficient = numer / (denom + epsilon_den)
    eddy = coefficient * width_sq * magnitude(tensor)
    stress = 2.0 * (nu_molecular + coefficient * width_sq * magnitude(tensor_wide)) * tensor_wide
    predicted_cycle = interior(interior(wide_faces)) + time_step * divergence(stress, radius)
    source = continuity(predicted_cycle, radius)
    tiles = source.reshape(LOCAL_T, 8, 4, NR).transpose(3, 1, 2, 0).reshape(NR, 8, 128)
    pressure = solve(spectral(tiles))
    return (eddy / nu_molecular, pressure)


def solution(mesh):
    return jax.shard_map(
        body,
        mesh=mesh,
        in_specs=(P(None, "theta", "gz", None),),
        out_specs=(P("theta", "gz", None), P(None, "gz", "theta", None)),
        check_vma=False,
    )
```

profile of v0, /device:TPU:1, one launch (start us, length us, event | category | flops | bytes accessed | tf_op | source)
XLA Modules:
  0.0 192.5 jit_solution(18130611754549925890)
XLA Ops:
  0.6 1.0 fusion.76
  1.6 4.2 %collective-permute-start = (f32[3,3,32,128]{3,2,1,0:T(8,128)S(1)}, f32[3,3,32,128]{3,2,1,0:T(8,128)S(1)}, u32[]{:S(2)}, u32[]{:S(2)}) collective-permute-start(f32[3,3,32,128]{3,2,1,0:T(8,128)S(1)} %get-tuple-element.30), channel_id=1, source_target_pairs={{0,8},{8,16},{16,24},{24,32},{32,40},{40,48},{48,56},{56,64},{64,7... | collective-permute-start | bytes 442376 | tf_op jit(solution)/shard_map/ppermute | solution.py:33
  5.8 0.0 collective-permute-start.1
  5.8 2.1 %collective-permute-done = f32[3,3,32,128]{3,2,1,0:T(8,128)S(1)} collective-permute-done((f32[3,3,32,128]{3,2,1,0:T(8,128)S(1)}, f32[3,3,32,128]{3,2,1,0:T(8,128)S(1)}, u32[]{:S(2)}, u32[]{:S(2)}) %collective-permute-start) | collective-permute-done | bytes 147488 | tf_op jit(solution)/shard_map/ppermute | solution.py:33
  8.0 1.5 constant_dynamic-update-slice_fusion.1
  9.5 2.4 %collective-permute-done.1 = f32[3,3,32,128]{3,2,1,0:T(8,128)S(1)} collective-permute-done((f32[3,3,32,128]{3,2,1,0:T(8,128)S(1)}, f32[3,3,32,128]{3,2,1,0:T(8,128)S(1)}, u32[]{:S(2)}, u32[]{:S(2)}) %collective-permute-start.1) | collective-permute-done | bytes 147488 | tf_op jit(solution)/shard_map/ppermute | solution.py:36
  11.9 0.1 fusion.75
  12.0 3.3 %collective-permute-start.3 = (f32[3,38,3,128]{3,2,1,0:T(4,128)S(1)}, f32[3,38,3,128]{3,2,1,0:T(4,128)S(1)}, u32[]{:S(2)}, u32[]{:S(2)}) collective-permute-start(f32[3,38,3,128]{3,2,1,0:T(4,128)S(1)} %get-tuple-element.28), channel_id=1, source_target_pairs={{1,0},{2,1},{3,2},{4,3},{5,4},{6,5},{7,6},{0,7},{9,8},{10,9},{11,1... | collective-permute-start | bytes 525320 | tf_op jit(solution)/shard_map/ppermute | solution.py:36
  15.4 0.0 collective-permute-start.2
  15.4 3.5 %collective-permute-done.3 = f32[3,38,3,128]{3,2,1,0:T(4,128)S(1)} collective-permute-done((f32[3,38,3,128]{3,2,1,0:T(4,128)S(1)}, f32[3,38,3,128]{3,2,1,0:T(4,128)S(1)}, u32[]{:S(2)}, u32[]{:S(2)}) %collective-permute-start.3) | collective-permute-done | bytes 175136 | tf_op jit(solution)/shard_map/ppermute | solution.py:36
  18.9 4.0 %collective-permute-done.2 = f32[3,38,3,128]{3,2,1,0:T(4,128)S(1)} collective-permute-done((f32[3,38,3,128]{3,2,1,0:T(4,128)S(1)}, f32[3,38,3,128]{3,2,1,0:T(4,128)S(1)}, u32[]{:S(2)}, u32[]{:S(2)}) %collective-permute-start.2) | collective-permute-done | bytes 175136 | tf_op jit(solution)/shard_map/ppermute | solution.py:33
  23.0 0.4 pad_maximum_fusion
  23.4 1.5 slice_dynamic-update-slice_fusion.1
  24.9 0.7 fusion.16
  25.6 0.0 copy-start.3
  25.6 1.2 fusion.15
  26.8 0.0 copy-start.4
  26.8 0.1 constant_dynamic-update-slice_fusion.6
  27.0 0.1 slice_dynamic-update-slice_fusion.2
  27.0 0.2 constant_dynamic-update-slice_fusion.5
  27.2 0.0 copy-start.9
  27.2 0.1 constant_dynamic-update-slice_fusion.4
  27.3 0.0 copy-start.5
  27.3 0.1 constant_dynamic-update-slice_fusion.3
  27.4 0.0 copy-start.7
  27.5 0.0 copy-start.2
  27.5 1.4 multiply_dynamic-update-slice_fusion.6
  28.9 1.5 multiply_dynamic-update-slice_fusion.5
  30.3 0.9 multiply_dynamic-update-slice_fusion.4
  31.2 1.0 multiply_dynamic-update-slice_fusion.3
  32.2 1.0 multiply_dynamic-update-slice_fusion.2
  33.3 1.0 multiply_dynamic-update-slice_fusion.1
  34.3 2.4 %slice_dynamic-update-slice_fusion = f32[21,34,34,128]{3,2,1,0:T(8,128)} fusion(f32[21,34,34,128]{3,2,1,0:T(8,128)} %multiply_dynamic-update-slice_fusion.1, f32[6,36,36,128]{3,2,1,0:T(8,128)S(1)} %get-tuple-element.6), kind=kLoop, calls=%fused_computation.23 | loop fusion | bytes 7729152
  36.7 0.0 copy-done.3
  36.7 0.7 fusion.34
  37.5 2.5 %multiply_dynamic-update-slice_fusion = f32[21,34,34,128]{3,2,1,0:T(8,128)} fusion(f32[21,34,34,128]{3,2,1,0:T(8,128)} %slice_dynamic-update-slice_fusion, f32[6,36,36,128]{3,2,1,0:T(8,128)S(1)} %get-tuple-element.6, f32[34,34,128]{2,1,0:T(8,128)S(1)} %fusion.34), kind=kLoop, calls=%fused_computation.22 | loop fusion | flops 887808 | bytes 8321024 | tf_op jit(solution)/shard_map/concatenate | solution.py:108
  39.9 13.9 %fusion = f32[21,32,34,128]{3,2,1,0:T(8,128)S(1)} fusion(f32[21,34,34,128]{3,2,1,0:T(8,128)} %multiply_dynamic-update-slice_fusion), kind=kLoop, calls=%fused_computation.1 | loop fusion | flops 14622720 | bytes 46792704 | tf_op jit(solution)/shard_map/add | solution.py:94
  53.9 5.8 %fusion.2 = f32[21,32,32,128]{3,2,1,0:T(8,128)} fusion(f32[21,32,34,128]{3,2,1,0:T(8,128)S(1)} %fusion), kind=kLoop, calls=%fused_computation.6 | loop fusion | flops 13762560 | bytes 44040192 | tf_op jit(solution)/shard_map/add | solution.py:97
  59.7 1.2 multiply_dynamic-update-slice_fusion.12
  61.0 1.3 multiply_dynamic-update-slice_fusion.11
  62.3 1.5 multiply_dynamic-update-slice_fusion.10
  63.8 0.0 copy-start.11
  63.8 1.3 multiply_dynamic-update-slice_fusion.9
  65.1 1.3 multiply_dynamic-update-slice_fusion.8
  66.3 2.7 %multiply_dynamic-update-slice_fusion.7 = (f32[6,32,32,128]{3,2,1,0:T(8,128)S(1)}, f32[32,32,128]{2,1,0:T(8,128)S(1)}) fusion(f32[6,32,32,128]{3,2,1,0:T(8,128)S(1)} %multiply_dynamic-update-slice_fusion.8, f32[21,32,32,128]{3,2,1,0:T(8,128)} %fusion.2), kind=kLoop, calls=%fused_computation.141 | loop fusion | flops 1966080 | bytes 5242880 | tf_op jit(solution)/shard_map/stack | solution.py:113
  69.1 1.8 fusion.9
  70.9 67.2 %all-reduce.6 = (f32[128]{0:T(128)S(1)}, f32[128]{0:T(128)S(1)}) all-reduce(f32[128]{0:T(128)S(1)} %get-tuple-element.3, f32[128]{0:T(128)S(1)} %get-tuple-element.2), channel_id=1, replica_groups=mesh['theta'=16,'gz'=8] {'theta','gz'}, use_global_device_ids=true, to_apply=%region_1.0 | all-reduce | flops 256 | bytes 2048 | tf_op jit(solution)/shard_map/psum | solution.py:451
  138.1 3.4 %fusion.54 = f32[32,32,128]{2,1,0:T(8,128)} fusion(f32[1,36,36,128]{3,2,1,0:T(8,128)} %copy-done.7, f32[1,36,36,128]{3,2,1,0:T(8,128)} %copy-done.5, f32[1,36,36,128]{3,2,1,0:T(8,128)} %copy-done.9, f32[3,36,36,128]{3,2,1,0:T(8,128)} %copy-done.3, f32[1,36,36,128]{3,2,1,0:T(8,128)S(1)} %get-tuple-element.13, f32[3,36,36,128]{3,2,1,0:T(8,128)} %copy-done.4, ...), kind=kLoop, calls=%fused_computation.115 | loop fusion | flops 1966080 | bytes 3670528 | tf_op jit(solution)/shard_map/div | solution.py:459
  141.6 0.0 copy-done.8
  141.6 1.9 multiply_bitcast_fusion
  143.5 2.6 %broadcast_multiply_fusion = f32[6,36,36,128]{3,2,1,0:T(8,128)S(1)} fusion(f32[6,36,36,128]{3,2,1,0:T(8,128)} %copy-done.2, f32[36,36,128]{2,1,0:T(8,128)S(1)} %multiply_bitcast_fusion), kind=kLoop, calls=%fused_computation.40 | loop fusion | flops 995328 | bytes 8626176 | tf_op jit(solution)/shard_map/mul | solution.py:454
  146.1 2.2 %fusion.74 = (f32[6,34,34,128]{3,2,1,0:T(8,128)S(1)}, f32[6,34,34,128]{3,2,1,0:T(8,128)S(1)}, f32[6,34,34,128]{3,2,1,0:T(8,128)S(1)}) fusion(f32[6,36,36,128]{3,2,1,0:T(8,128)S(1)} %broadcast_multiply_fusion, f32[128]{0:T(128)S(1)} %fusion.69), kind=kLoop, calls=%fused_computation.159 | loop fusion | flops 4439040 | bytes 28410368 | tf_op jit(solution)/shard_map/slice | solution.py:65
  148.3 2.2 %fusion.5 = f32[6,34,34,128]{3,2,1,0:T(8,128)S(1)} fusion(f32[6,34,34,128]{3,2,1,0:T(8,128)S(1)} %get-tuple-element.19), kind=kLoop, calls=%fused_computation.16 | loop fusion | flops 1775616 | bytes 7102464 | tf_op jit(solution)/shard_map/mul | solution.py:61
  150.6 0.6 fusion.29
  151.2 0.4 fusion.19
  151.6 0.1 fusion.47
  151.7 0.0 copy-start
  151.7 0.1 slice_bitcast_fusion.1
  151.8 0.4 fusion.43
  152.1 0.3 copy.7
  152.5 0.2 copy.8.tiles_ref
  152.7 0.1 copy-done
  152.8 36.4 %spectral.1.modes_ref = f32[128,16,128]{2,1,0:T(8,128)S(1)} custom-call(f32[128,8,128]{2,1,0:T(8,128)S(1)} %copy.8.tiles_ref, bf16[3,512,256]{2,1,0:T(8,128)(2,1)S(1)} %copy-done, bf16[3,4,1024,256]{3,2,1,0:T(8,128)(2,1)} %constant.31.clone.cycle_hbm), custom_call_target="tpu_custom_call" | custom-call | tf_op jit(solution)/shard_map/spectral/pallas_call | solution.py:350
  189.2 3.3 %solve.1 = f32[128,16,128]{2,1,0:T(8,128)} custom-call(f32[128,16,128]{2,1,0:T(8,128)S(1)} %spectral.1.modes_ref), custom_call_target="tpu_custom_call" | custom-call | tf_op jit(solution)/shard_map/solve/pallas_call | solution.py:430
  (19 shorter events, 0.2 us)
Async XLA Ops:
  1.6 6.3 %collective-permute-start = (f32[3,3,32,128]{3,2,1,0:T(8,128)S(1)}, f32[3,3,32,128]{3,2,1,0:T(8,128)S(1)}, u32[]{:S(2)}, u32[]{:S(2)}) collective-permute-start(f32[3,3,32,128]{3,2,1,0:T(8,128)S(1)} %get-tuple-element.30), channel_id=1, source_target_pairs={{0,8},{8,16},{16,24},{24,32},{32,40},{40,48},{48,56},{56,64},{64,7... | collective-permute-start | bytes 442376 | tf_op jit(solution)/shard_map/ppermute | solution.py:33
  5.8 6.1 %collective-permute-start.1 = (f32[3,3,32,128]{3,2,1,0:T(8,128)S(1)}, f32[3,3,32,128]{3,2,1,0:T(8,128)S(1)}, u32[]{:S(2)}, u32[]{:S(2)}) collective-permute-start(f32[3,3,32,128]{3,2,1,0:T(8,128)S(1)} %get-tuple-element.29), channel_id=1, source_target_pairs={{8,0},{16,8},{24,16},{32,24},{40,32},{48,40},{56,48},{64,56},{72,6... | collective-permute-start | bytes 442376 | tf_op jit(solution)/shard_map/ppermute | solution.py:36
  12.0 6.9 %collective-permute-start.3 = (f32[3,38,3,128]{3,2,1,0:T(4,128)S(1)}, f32[3,38,3,128]{3,2,1,0:T(4,128)S(1)}, u32[]{:S(2)}, u32[]{:S(2)}) collective-permute-start(f32[3,38,3,128]{3,2,1,0:T(4,128)S(1)} %get-tuple-element.28), channel_id=1, source_target_pairs={{1,0},{2,1},{3,2},{4,3},{5,4},{6,5},{7,6},{0,7},{9,8},{10,9},{11,1... | collective-permute-start | bytes 525320 | tf_op jit(solution)/shard_map/ppermute | solution.py:36
  15.4 7.6 %collective-permute-start.2 = (f32[3,38,3,128]{3,2,1,0:T(4,128)S(1)}, f32[3,38,3,128]{3,2,1,0:T(4,128)S(1)}, u32[]{:S(2)}, u32[]{:S(2)}) collective-permute-start(f32[3,38,3,128]{3,2,1,0:T(4,128)S(1)} %get-tuple-element.27), channel_id=1, source_target_pairs={{0,1},{1,2},{2,3},{3,4},{4,5},{5,6},{6,7},{7,0},{8,9},{9,10},{10,1... | collective-permute-start | bytes 525320 | tf_op jit(solution)/shard_map/ppermute | solution.py:33
  25.6 11.1 %copy-start.3 = (f32[3,36,36,128]{3,2,1,0:T(8,128)}, f32[3,36,36,128]{3,2,1,0:T(8,128)S(1)}, u32[]{:S(2)}) copy-start(f32[3,36,36,128]{3,2,1,0:T(8,128)S(1)} %get-tuple-element.22) | copy-start | bytes 5971972
  26.8 9.9 %copy-start.4 = (f32[3,36,36,128]{3,2,1,0:T(8,128)}, f32[3,36,36,128]{3,2,1,0:T(8,128)S(1)}, u32[]{:S(2)}) copy-start(f32[3,36,36,128]{3,2,1,0:T(8,128)S(1)} %fusion.15) | copy-start | bytes 5971972
  27.2 9.5 %copy-start.9 = (f32[1,36,36,128]{3,2,1,0:T(8,128)}, f32[1,36,36,128]{3,2,1,0:T(8,128)S(1)}, u32[]{:S(2)}) copy-start(f32[1,36,36,128]{3,2,1,0:T(8,128)S(1)} %get-tuple-element.11) | copy-start | bytes 1990660
  27.3 9.4 %copy-start.5 = (f32[1,36,36,128]{3,2,1,0:T(8,128)}, f32[1,36,36,128]{3,2,1,0:T(8,128)S(1)}, u32[]{:S(2)}) copy-start(f32[1,36,36,128]{3,2,1,0:T(8,128)S(1)} %get-tuple-element.9) | copy-start | bytes 1990660
  27.4 9.3 %copy-start.7 = (f32[1,36,36,128]{3,2,1,0:T(8,128)}, f32[1,36,36,128]{3,2,1,0:T(8,128)S(1)}, u32[]{:S(2)}) copy-start(f32[1,36,36,128]{3,2,1,0:T(8,128)S(1)} %get-tuple-element.7) | copy-start | bytes 1990660
  27.5 10.0 %copy-start.2 = (f32[6,36,36,128]{3,2,1,0:T(8,128)}, f32[6,36,36,128]{3,2,1,0:T(8,128)S(1)}, u32[]{:S(2)}) copy-start(f32[6,36,36,128]{3,2,1,0:T(8,128)S(1)} %get-tuple-element.6) | copy-start | bytes 11943940
  59.7 9.3 %copy-start.1 = (f32[21,32,32,128]{3,2,1,0:T(8,128)S(1)}, f32[21,32,32,128]{3,2,1,0:T(8,128)}, u32[]{:S(2)}) copy-start(f32[21,32,32,128]{3,2,1,0:T(8,128)} %fusion.2) | copy-start | bytes 33030148
  63.8 5.3 %copy-start.11 = (f32[6]{0:T(128)S(1)}, f32[6]{0:T(128)}, u32[]{:S(2)}) copy-start(f32[6]{0:T(128)} %constant.29.clone) | copy-start | bytes 76
  138.1 3.5 %copy-start.6 = (f32[1,36,36,128]{3,2,1,0:T(8,128)S(1)}, f32[1,36,36,128]{3,2,1,0:T(8,128)}, u32[]{:S(2)}) copy-start(f32[1,36,36,128]{3,2,1,0:T(8,128)} %copy-done.5) | copy-start | bytes 1990660
  138.1 3.5 %copy-start.8 = (f32[1,36,36,128]{3,2,1,0:T(8,128)S(1)}, f32[1,36,36,128]{3,2,1,0:T(8,128)}, u32[]{:S(2)}) copy-start(f32[1,36,36,128]{3,2,1,0:T(8,128)} %copy-done.7) | copy-start | bytes 1990660
  138.1 3.5 %copy-start.10 = (f32[1,36,36,128]{3,2,1,0:T(8,128)S(1)}, f32[1,36,36,128]{3,2,1,0:T(8,128)}, u32[]{:S(2)}) copy-start(f32[1,36,36,128]{3,2,1,0:T(8,128)} %copy-done.9) | copy-start | bytes 1990660
  151.7 1.1 copy-start
where the time goes:
time: 193 us
  blocking collectives  67.2 us (35%)
  other arithmetic  57.5 us (30%)
  Pallas kernels  39.7 us (21%)
  waiting for transfers between devices  12.1 us (6%)
  starting transfers between devices  7.55 us (4%)
  local copies, waits for them, and re-layouts  7.5 us (4%)
    psum x1, blocking collectives, body(): numer, denom = lax.psum((numer, denom), ('theta', 'gz'))  67.2 us
    pallas_call x1, Pallas kernels, spectral(): pl.pallas_call(spectral_kernel, out_shape=jax.ShapeDtypeStruct((DEVICES,...  36.4 us
    add x1, other arithmetic, test_filter(): 0.25 * padded[..., :-2, :, :] + 0.5 * padded[..., 1:-1, :, :]  13.9 us
    unnamed x14, other arithmetic  13.7 us
    ppermute x2, waiting for transfers between devices, with_halo(): lax.ppermute(lax.slice_in_dim(block, block.shape[dim] - width, None, axis...  6.13 us
    ppermute x2, waiting for transfers between devices, with_halo(): lax.ppermute(lax.slice_in_dim(block, 0, width, axis=dim), axis, backward)  5.94 us
    add x1, other arithmetic, test_filter(): 0.25 * across[..., :, :-2, :] + 0.5 * across[..., :, 1:-1, :]  5.84 us
    unnamed x30, local copies, waits for them, and re-layouts  5.77 us
  transfers between devices with their start and end apart: 4, of which 4 were waited for; matrix products, arithmetic and copies ran while one was open for 1% of the time, Pallas kernels for 0%

commit v1 on v0

--- a/solution.py
+++ b/solution.py
@@ -22,131 +22,6 @@
 epsilon_den = 1e-06
 pair_first = (0, 1, 2, 0, 0, 1)
 pair_second = (0, 1, 2, 1, 2, 2)
-
-
-def with_halo(block, sides, width):
-    for axis, dim in sides:
-        count = lax.axis_size(axis)
-        forward = [(i, i + 1) for i in range(count - 1)]
-        forward.append((count - 1, 0))
-        backward = [(target, source) for source, target in forward]
-        low = lax.ppermute(
-            lax.slice_in_dim(block, block.shape[dim] - width, None, axis=dim), axis, forward
-        )
-        high = lax.ppermute(lax.slice_in_dim(block, 0, width, axis=dim), axis, backward)
-        block = jnp.concatenate([low, block, high], axis=dim)
-    return block
-
-
-def grid_terms():
-    radial_step = 1.0 / NR
-    radius = (jnp.arange(NR, dtype=jnp.float32) + 0.5) * radial_step
-    theta_step = 2.0 * math.pi / NTH
-    axial_step = pipe_length / NZ
-    width_sq = jnp.cbrt(radial_step * radius * theta_step * axial_step) ** 2
-    return (radius, width_sq)
-
-
-def along_theta(padded):
-    return (padded[..., 2:, 1:-1, :] - padded[..., :-2, 1:-1, :]) * (0.5 * NTH / (2.0 * math.pi))
-
-
-def along_axis(padded):
-    return (padded[..., 1:-1, 2:, :] - padded[..., 1:-1, :-2, :]) * (0.5 * NZ / pipe_length)
-
-
-def along_radius(field):
-    zeros = jnp.zeros(field.shape[:-1] + (1,), field.dtype)
-    extended = jnp.concatenate([zeros, field, zeros], axis=-1)
-    return (extended[..., 2:] - extended[..., :-2]) * (0.5 * NR)
-
-
-def interior(padded):
-    return padded[..., 1:-1, 1:-1, :]
-
-
-def strain(padded, radius):
-    centre = interior(padded)
-    radial = along_radius(centre)
-    azimuthal = along_theta(padded) / radius
-    axial = along_axis(padded)
-    return jnp.stack(
-        [
-            radial[0],
-            azimuthal[1] + centre[0] / radius,
-            axial[2],
-            0.5 * (radial[1] - centre[1] / radius + azimuthal[0]),
-            0.5 * (axial[0] + radial[2]),
-            0.5 * (azimuthal[2] + axial[1]),
-        ]
-    )
-
-
-def magnitude(tensor):
-    return jnp.sqrt(
-        2.0 * (tensor[0] ** 2 + tensor[1] ** 2 + tensor[2] ** 2)
-        + 4.0 * (tensor[3] ** 2 + tensor[4] ** 2 + tensor[5] ** 2)
-    )
-
-
-def test_filter(padded):
-    across = (
-        0.25 * padded[..., :-2, :, :] + 0.5 * padded[..., 1:-1, :, :] + 0.25 * padded[..., 2:, :, :]
-    )
-    return (
-        0.25 * across[..., :, :-2, :] + 0.5 * across[..., :, 1:-1, :] + 0.25 * across[..., :, 2:, :]
-    )
-
-
-def products(flow, tensor):
-    pairs = jnp.stack(
-        [
-            flow[first_comp] * flow[second_comp]
-            for first_comp, second_comp in zip(pair_first, pair_second)
-        ]
-    )
-    return jnp.concatenate([flow, pairs, tensor, magnitude(tensor) * tensor], axis=0)
-
-
-def germano(filtered, width_sq):
-    means = filtered[0:3]
-    pairs = jnp.stack(
-        [
-            means[first_comp] * means[second_comp]
-            for first_comp, second_comp in zip(pair_first, pair_second)
-        ]
-    )
-    leonard = filtered[3:9] - pairs
-    smooth = filtered[9:15]
-    model = 2.0 * width_sq * (filter_ratio * magnitude(smooth) * smooth - filtered[15:21])
-    weights = jnp.array([1.0, 1.0, 1.0, 2.0, 2.0, 2.0], dtype=jnp.float32)[:, None, None, None]
-    return (
-        jnp.sum(weights * leonard * model, axis=(0, 1, 2)),
-        jnp.sum(weights * model * model, axis=(0, 1, 2)),
-    )
-
-
-def divergence(stress, radius):
-    centre = interior(stress)
-    radial = along_radius(centre)
-    azimuthal = along_theta(stress) / radius
-    axial = along_axis(stress)
-    return jnp.stack(
-        [
-            radial[0] + azimuthal[3] + axial[4] + (centre[0] - centre[1]) / radius,
-            radial[3] + azimuthal[1] + axial[5] + 2.0 * centre[3] / radius,
-            radial[4] + azimuthal[5] + axial[2] + centre[4] / radius,
-        ]
-    )
-
-
-def continuity(padded, radius):
-    centre = interior(padded)
-    return (
-        along_radius(radius * centre[0]) / radius
-        + along_theta(padded[1]) / radius
-        + along_axis(padded[2])
-    )
 
 
 THETA_COUNT = 16
@@ -160,6 +35,381 @@
 HALF = NR // 2
 
 
+def wait_bytes(ref, sem):
+    pltpu.make_async_copy(ref, ref, sem).wait()
+
+
+T_ROWS = LOCAL_T + 6
+Z_BASE = 8
+Z_ROWS = LOCAL_Z + 2 * Z_BASE
+Z_STEP = LOCAL_Z // 8
+S_ROWS = LOCAL_T + 4
+S_COLS = Z_STEP + 4
+DT = 0.5 * NTH / (2.0 * math.pi)
+DZ = 0.5 * NZ / pipe_length
+
+
+def radial_table():
+    radius = (np.arange(NR) + 0.5) / NR
+    width = np.cbrt((1.0 / NR) * radius * (2.0 * np.pi / NTH) * (pipe_length / NZ)) ** 2
+    upper = np.full(NR, 0.5 * NR)
+    lower = upper.copy()
+    upper[-1] = 0.0
+    lower[0] = 0.0
+    rows = np.stack([1.0 / radius, DT / radius, upper, lower, width, radius])
+    return np.broadcast_to(rows[:, None, :], (6, 8, NR)).astype(np.float32)
+
+
+def along_radius(field, radial):
+    return pltpu.roll(field, NR - 1, 1) * radial[2] - pltpu.roll(field, 1, 1) * radial[3]
+
+
+def tensor_magnitude(t):
+    diagonal = t[0] * t[0] + t[1] * t[1] + t[2] * t[2]
+    mixed = t[3] * t[3] + t[4] * t[4] + t[5] * t[5]
+    return jnp.sqrt(2.0 * diagonal + 4.0 * mixed)
+
+
+def neighbours(row, column):
+    below, above = lax.rem(row + THETA_COUNT - 1, THETA_COUNT), lax.rem(row + 1, THETA_COUNT)
+    left, right = lax.rem(column + GZ_COUNT - 1, GZ_COUNT), lax.rem(column + 1, GZ_COUNT)
+    return below, above, left, right
+
+
+def device(row, column):
+    return {"theta": row, "gz": column}
+
+
+def exchange(velocity, flow, packed, landed, load_sem, send_sem, recv_sem, barrier):
+    row, column = lax.axis_index("theta"), lax.axis_index("gz")
+    below, above, left, right = neighbours(row, column)
+    load = pltpu.make_async_copy(
+        velocity, flow.at[:, pl.ds(3, LOCAL_T), pl.ds(Z_BASE, LOCAL_Z), :], load_sem
+    )
+    load.start()
+
+    def greet_row(i, carry):
+        target = lax.rem(row + i, THETA_COUNT)
+        pl.semaphore_signal(barrier, inc=1, device_id=device(target, column), device_id_type=MESH_ID)
+        return carry
+
+    def greet_column(i, carry):
+        target = lax.rem(column + i, GZ_COUNT)
+        pl.semaphore_signal(barrier, inc=1, device_id=device(row, target), device_id_type=MESH_ID)
+        return carry
+
+    lax.fori_loop(1, THETA_COUNT, greet_row, 0)
+    lax.fori_loop(1, GZ_COUNT, greet_column, 0)
+    for r in (below, above):
+        for c in (left, right):
+            pl.semaphore_signal(barrier, inc=1, device_id=device(r, c), device_id_type=MESH_ID)
+    pl.semaphore_wait(barrier, THETA_COUNT + GZ_COUNT + 2)
+
+    def copy(n, source, target, r, c):
+        return pltpu.make_async_remote_copy(
+            src_ref=source,
+            dst_ref=target,
+            send_sem=send_sem.at[n],
+            recv_sem=recv_sem.at[n],
+            device_id=device(r, c),
+            device_id_type=MESH_ID,
+        )
+
+    inner = pl.ds(Z_BASE, LOCAL_Z)
+    copies = [
+        copy(0, velocity.at[:, pl.ds(LOCAL_T - 3, 3)], flow.at[:, pl.ds(0, 3), inner], above, column),
+        copy(1, velocity.at[:, pl.ds(0, 3)], flow.at[:, pl.ds(LOCAL_T + 3, 3), inner], below, column),
+    ]
+    for item in copies:
+        item.start()
+    load.wait()
+    for side, first in ((0, Z_BASE + LOCAL_Z - 3), (1, Z_BASE)):
+        for comp in range(3):
+            for z in range(3):
+                packed[side, 3 * comp + z] = flow[comp, pl.ds(3, LOCAL_T), first + z, :]
+    for side, target in ((0, right), (1, left)):
+        main, low, high = pl.ds(8, LOCAL_T), pl.ds(0, 8), pl.ds(LOCAL_T + 8, 8)
+        sides = [
+            copy(2 + 3 * side, packed.at[side], landed.at[side, :, main], row, target),
+            copy(3 + 3 * side, packed.at[side, :, pl.ds(LOCAL_T - 8, 8)], landed.at[side, :, low], above, target),
+            copy(4 + 3 * side, packed.at[side, :, pl.ds(0, 8)], landed.at[side, :, high], below, target),
+        ]
+        for item in sides:
+            item.start()
+        copies += sides
+    for item in copies:
+        item.wait()
+    for side, first in ((0, Z_BASE - 3), (1, Z_BASE + LOCAL_Z)):
+        for comp in range(3):
+            for z in range(3):
+                flow[comp, :, first + z, :] = landed[side, 3 * comp + z, pl.ds(5, T_ROWS), :]
+
+
+def read_flow(flow, comp, t, q):
+    return flow[comp, t, pl.ds(Z_BASE + q, 8, stride=Z_STEP), :]
+
+
+def strain_rows(flow, tensor, radial):
+    def strain_row(n, carry):
+        centre = [[read_flow(flow, c, n + 1, q) for q in range(-3, Z_STEP + 3)] for c in range(3)]
+        for i in range(S_COLS):
+            u = [centre[c][i + 1] for c in range(3)]
+            dz = [(centre[c][i + 2] - centre[c][i]) * DZ for c in range(3)]
+            dt = [
+                (read_flow(flow, c, n + 2, i - 2) - read_flow(flow, c, n, i - 2)) * radial[1]
+                for c in range(3)
+            ]
+            dr = [along_radius(u[c], radial) for c in range(3)]
+            parts = [
+                dr[0],
+                dt[1] + u[0] * radial[0],
+                dz[2],
+                0.5 * (dr[1] - u[1] * radial[0] + dt[0]),
+                0.5 * (dz[0] + dr[2]),
+                0.5 * (dt[2] + dz[1]),
+            ]
+            for k in range(6):
+                tensor[k, n, i] = parts[k]
+            tensor[6, n, i] = tensor_magnitude(parts)
+        return carry
+
+    lax.fori_loop(0, S_ROWS, strain_row, 0)
+
+
+def filter_rows(flow, tensor, state, filtered):
+    span = range(-1, Z_STEP + 1)
+
+    def across(n):
+        flows = [[read_flow(flow, c, n + 1, q) for q in span] for c in range(3)]
+        for c in range(3):
+            yield flows[c]
+        for a, b in zip(pair_first, pair_second):
+            yield [x * y for x, y in zip(flows[a], flows[b])]
+        for k in range(6):
+            yield [tensor[k, n, q + 2] for q in span]
+        for k in range(6):
+            yield [tensor[k, n, q + 2] * tensor[6, n, q + 2] for q in span]
+
+    def axial(values):
+        pairs = [x + y for x, y in zip(values[:-1], values[1:])]
+        return [x + y for x, y in zip(pairs[:-1], pairs[1:])]
+
+    def first_rows():
+        for f, (one, two) in enumerate(zip(across(1), across(2))):
+            one, two = axial(one), axial(two)
+            for q in range(Z_STEP):
+                state[0, f, q] = two[q]
+                state[1, f, q] = one[q] + two[q]
+
+    def pair_rows(step, carry):
+        n = 3 + 2 * step
+        for f, (one, two) in enumerate(zip(across(n), across(n + 1))):
+            one, two = axial(one), axial(two)
+            for q in range(Z_STEP):
+                before = state[0, f, q] + one[q]
+                after = one[q] + two[q]
+                filtered[f, q] = state[1, f, q] + before
+                filtered[f, Z_STEP + q] = before + after
+                state[0, f, q] = two[q]
+                state[1, f, q] = after
+        numer, denom = carry
+        for q in range(2 * Z_STEP):
+            means = [filtered[c, q] for c in range(3)]
+            smooth = [filtered[9 + k, q] for k in range(6)]
+            size = tensor_magnitude(smooth) * (filter_ratio / 16.0)
+            lm, mm = [], []
+            for k in range(6):
+                leonard = filtered[3 + k, q] - means[pair_first[k]] * means[pair_second[k]] * (1.0 / 16.0)
+                model = size * smooth[k] - filtered[15 + k, q]
+                lm.append(leonard * model)
+                mm.append(model * model)
+            numer = numer + (lm[0] + lm[1] + lm[2]) + 2.0 * (lm[3] + lm[4] + lm[5])
+            denom = denom + (mm[0] + mm[1] + mm[2]) + 2.0 * (mm[3] + mm[4] + mm[5])
+        return numer, denom
+
+    first_rows()
+    zero = jnp.zeros((8, NR), jnp.float32)
+    return lax.fori_loop(0, LOCAL_T // 2, pair_rows, (zero, zero))
+
+
+def sum_everywhere(numer, denom, row_sums, all_sums, send_sem, recv_sem):
+    row, column = lax.axis_index("theta"), lax.axis_index("gz")
+    first = lax.broadcasted_iota(jnp.int32, (8, NR), 0) == 0
+    tile = jnp.where(
+        first, jnp.sum(numer, axis=0, keepdims=True), jnp.sum(denom, axis=0, keepdims=True)
+    )
+
+    def share(buffer, tile, place, count, target, step):
+        buffer[place] = tile
+
+        def send(i, carry):
+            pltpu.make_async_remote_copy(
+                src_ref=buffer.at[place],
+                dst_ref=buffer.at[place],
+                send_sem=send_sem.at[step],
+                recv_sem=recv_sem.at[step],
+                device_id=target(lax.rem(place + i, count)),
+                device_id_type=MESH_ID,
+            ).start()
+            return carry
+
+        lax.fori_loop(1, count, send, 0)
+        others = buffer.at[pl.ds(0, count - 1)]
+        wait_bytes(others, recv_sem.at[step])
+        wait_bytes(others, send_sem.at[step])
+        total = buffer[0]
+        for i in range(1, count):
+            total = total + buffer[i]
+        return total
+
+    tile = share(row_sums, tile, row, THETA_COUNT, lambda i: device(i, column), 0)
+    tile = share(all_sums, tile, column, GZ_COUNT, lambda i: device(row, i), 1)
+    return tile[0:1], tile[1:2]
+
+
+def stress_rows(tensor, ratio, eddy):
+    def stress_row(n, carry):
+        for i in range(S_COLS):
+            viscosity = eddy * tensor[6, n, i]
+            scale = 2.0 * viscosity + 2.0 * nu_molecular
+            for k in range(6):
+                tensor[k, n, i] = tensor[k, n, i] * scale
+        return carry
+
+    def ratio_row(t, carry):
+        for q in range(Z_STEP):
+            value = eddy * tensor[6, t + 2, q + 2] * (1.0 / nu_molecular)
+            ratio[t, pl.ds(q, 8, stride=Z_STEP), :] = value
+        return carry
+
+    lax.fori_loop(0, LOCAL_T, ratio_row, 0)
+    lax.fori_loop(0, S_ROWS, stress_row, 0)
+
+
+def source_rows(flow, tensor, swirl, partial, source, radial):
+    def swirl_row(n, carry):
+        for q in range(Z_STEP):
+            i = q + 2
+            shear = tensor[3, n, i]
+            force = (
+                along_radius(shear, radial)
+                + (tensor[1, n + 1, i] - tensor[1, n - 1, i]) * radial[1]
+                + (tensor[5, n, i + 1] - tensor[5, n, i - 1]) * DZ
+                + 2.0 * shear * radial[0]
+            )
+            swirl[n - 1, q] = read_flow(flow, 1, n + 1, q) + time_step * force
+        return carry
+
+    def other_row(t, carry):
+        n = t + 2
+        axial = []
+        for q in range(-1, Z_STEP + 1):
+            i = q + 2
+            shear = tensor[4, n, i]
+            force = (
+                along_radius(shear, radial)
+                + (tensor[5, n + 1, i] - tensor[5, n - 1, i]) * radial[1]
+                + (tensor[2, n, i + 1] - tensor[2, n, i - 1]) * DZ
+                + shear * radial[0]
+            )
+            axial.append(read_flow(flow, 2, n + 1, q) + time_step * force)
+        for q in range(Z_STEP):
+            i = q + 2
+            normal = tensor[0, n, i]
+            force = (
+                along_radius(normal, radial)
+                + (tensor[3, n + 1, i] - tensor[3, n - 1, i]) * radial[1]
+                + (tensor[4, n, i + 1] - tensor[4, n, i - 1]) * DZ
+                + (normal - tensor[1, n, i]) * radial[0]
+            )
+            outward = (read_flow(flow, 0, n + 1, q) + time_step * force) * radial[5]
+            partial[t, q] = along_radius(outward, radial) * radial[0] + (axial[q + 2] - axial[q]) * DZ
+        return carry
+
+    def join_row(t, carry):
+        for q in range(Z_STEP):
+            value = partial[t, q] + (swirl[t + 2, q] - swirl[t, q]) * radial[1]
+            source[:, q * LOCAL_T + t, :] = value
+        return carry
+
+    lax.fori_loop(1, S_ROWS - 1, swirl_row, 0)
+    lax.fori_loop(0, LOCAL_T, other_row, 0)
+    lax.fori_loop(0, LOCAL_T, join_row, 0)
+
+
+def front_kernel(
+    velocity,
+    radial,
+    ratio,
+    tiles,
+    flow,
+    packed,
+    landed,
+    tensor,
+    state,
+    filtered,
+    row_sums,
+    all_sums,
+    swirl,
+    partial,
+    source,
+    load_sem,
+    send_sem,
+    recv_sem,
+    sum_send_sem,
+    sum_recv_sem,
+):
+    barrier = pltpu.get_barrier_semaphore()
+    exchange(velocity, flow, packed, landed, load_sem, send_sem, recv_sem, barrier)
+    strain_rows(flow, tensor, radial)
+    numer, denom = filter_rows(flow, tensor, state, filtered)
+    numer, denom = sum_everywhere(numer, denom, row_sums, all_sums, sum_send_sem, sum_recv_sem)
+    width = radial[4][0:1]
+    numer = numer * (width * (2.0 / 256.0))
+    denom = denom * (width * width * (4.0 / 256.0))
+    coefficient = numer / (denom + epsilon_den)
+    eddy = jnp.broadcast_to(coefficient * width, (8, NR))
+    stress_rows(tensor, ratio, eddy)
+    source_rows(flow, tensor, swirl, partial, source, radial)
+    for s in range(8):
+        tiles[:, s, :] = source[s].T
+
+
+def front(velocity):
+    vmem = pl.BlockSpec(memory_space=pltpu.VMEM)
+    return pl.pallas_call(
+        front_kernel,
+        out_shape=(
+            jax.ShapeDtypeStruct((LOCAL_T, LOCAL_Z, NR), jnp.float32),
+            jax.ShapeDtypeStruct((NR, 8, 4 * LOCAL_T), jnp.float32),
+        ),
+        in_specs=[pl.BlockSpec(memory_space=pl.ANY), vmem],
+        out_specs=(vmem, vmem),
+        scratch_shapes=[
+            pltpu.VMEM((3, T_ROWS, Z_ROWS, NR), jnp.float32),
+            pltpu.VMEM((2, 9, LOCAL_T, NR), jnp.float32),
+            pltpu.VMEM((2, 9, LOCAL_T + 16, NR), jnp.float32),
+            pltpu.VMEM((7, S_ROWS, S_COLS, 8, NR), jnp.float32),
+            pltpu.VMEM((2, 21, Z_STEP, 8, NR), jnp.float32),
+            pltpu.VMEM((21, 2 * Z_STEP, 8, NR), jnp.float32),
+            pltpu.VMEM((THETA_COUNT, 8, NR), jnp.float32),
+            pltpu.VMEM((GZ_COUNT, 8, NR), jnp.float32),
+            pltpu.VMEM((LOCAL_T + 2, Z_STEP, 8, NR), jnp.float32),
+            pltpu.VMEM((LOCAL_T, Z_STEP, 8, NR), jnp.float32),
+            pltpu.VMEM((8, 4 * LOCAL_T, NR), jnp.float32),
+            pltpu.SemaphoreType.DMA,
+            pltpu.SemaphoreType.DMA((8,)),
+            pltpu.SemaphoreType.DMA((8,)),
+            pltpu.SemaphoreType.DMA((2,)),
+            pltpu.SemaphoreType.DMA((2,)),
+        ],
+        compiler_params=pltpu.CompilerParams(
+            collective_id=1, has_side_effects=True, vmem_limit_bytes=48 << 20
+        ),
+        name="front",
+    )(velocity, jnp.asarray(radial_table()))
+
+
 def split_table(table):
     parts, rest = [], table
     for _ in range(3):
@@ -203,10 +453,6 @@
         term = jnp.dot(left[i], right[j], preferred_element_type=jnp.float32)
         total = term if total is None else total + term
     return total
-
-
-def wait_bytes(ref, sem):
-    pltpu.make_async_copy(ref, ref, sem).wait()
 
 
 def meet_all(row, column, barrier, second):
@@ -440,23 +686,8 @@
 
 
 def body(velocity):
-    radius, width_sq = grid_terms()
-    wide_faces = None
-    wide_faces = with_halo(velocity, (("theta", 1), ("gz", 2)), 3)
-    tensor_wide = strain(wide_faces, radius)
-    tensor_cycle = interior(tensor_wide)
-    filtered = test_filter(products(interior(interior(wide_faces)), tensor_cycle))
-    tensor = interior(tensor_cycle)
-    numer, denom = germano(filtered, width_sq)
-    numer, denom = lax.psum((numer, denom), ("theta", "gz"))
-    coefficient = numer / (denom + epsilon_den)
-    eddy = coefficient * width_sq * magnitude(tensor)
-    stress = 2.0 * (nu_molecular + coefficient * width_sq * magnitude(tensor_wide)) * tensor_wide
-    predicted_cycle = interior(interior(wide_faces)) + time_step * divergence(stress, radius)
-    source = continuity(predicted_cycle, radius)
-    tiles = source.reshape(LOCAL_T, 8, 4, NR).transpose(3, 1, 2, 0).reshape(NR, 8, 128)
-    pressure = solve(spectral(tiles))
-    return (eddy / nu_molecular, pressure)
+    ratio, tiles = front(velocity)
+    return (ratio, solve(spectral(tiles)))
 
 
 def solution(mesh):

time: 193 us -> 91.4 us (0.47)
  blocking collectives: 67.2 us -> 0 us
  other arithmetic: 57.5 us -> 0 us
  Pallas kernels: 39.7 us -> 86.5 us
  waiting for transfers between devices: 12.1 us -> 0 us
  starting transfers between devices: 7.55 us -> 0 us
  local copies, waits for them, and re-layouts: 7.5 us -> 4.06 us
    psum x1 -> x0, blocking collectives: 67.2 us -> none  [body(): numer, denom = lax.psum((numer, denom), ('theta', 'gz'))]
    pallas_call x0 -> x1, Pallas kernels: none -> 46.8 us  [front(): pl.pallas_call(front_kernel, out_shape=(jax.ShapeDtypeStruct((LOCAL_T, LO...]
    add x5 -> x0, other arithmetic: 21.2 us -> none  [the longest x1 13.9 us: test_filter(): 0.25 * padded[..., :-2, :, :] + 0.5 * padded[..., 1:-1, :, :]]
    unnamed x14 -> x0, other arithmetic: 13.7 us -> none
    ppermute x4 -> x0, waiting for transfers between devices: 12.1 us -> none  [the longest x2 6.13 us: with_halo(): lax.ppermute(lax.slice_in_dim(block, block.shape[dim] - width, None, axis...]
    mul x10 -> x0, other arithmetic: 9.48 us -> none  [the longest x2 4.55 us: body(): 2.0 * (nu_molecular + coefficient * width_sq * magnitude(tensor_wide))]
    ppermute x4 -> x0, starting transfers between devices: 7.55 us -> none  [the longest x2 4.21 us: with_halo(): lax.ppermute(lax.slice_in_dim(block, block.shape[dim] - width, None, axis...]
    div x1 -> x0, other arithmetic: 3.43 us -> none  [body(): return (eddy / nu_molecular, pressure)]
  transfers between devices with their start and end apart: 4 -> 0, of which waited for: 4 -> 0; matrix products, arithmetic and copies ran while one was open for 1% -> 0% of each run, Pallas kernels for 0% -> 0%
where the time goes in v1:
time: 91.4 us; the launch traced here: 91.2 us
  Pallas kernels  86.5 us (95%)
  local copies, waits for them, and re-layouts  4.06 us (4%)
    pallas_call x1, Pallas kernels, front(): pl.pallas_call(front_kernel, out_shape=(jax.ShapeDtypeStruct((LOCAL_T, LO...  46.8 us
    pallas_call x1, Pallas kernels, spectral(): pl.pallas_call(spectral_kernel, out_shape=jax.ShapeDtypeStruct((DEVICES,...  36.4 us
    unnamed x7, local copies, waits for them, and re-layouts  4.06 us
    pallas_call x1, Pallas kernels, solve(): pl.pallas_call(solve_kernel, out_shape=jax.ShapeDtypeStruct((2 * LOCAL_M,...  3.31 us

profile of v1, /device:TPU:1, one launch (start us, length us, event | category | flops | bytes accessed | tf_op | source)
XLA Modules:
  0.0 91.2 jit_solution(6990608676135238639)
XLA Ops:
  0.6 0.0 copy-start
  0.6 1.4 %copy-done = f32[3,32,32,128]{3,2,1,0:T(8,128)S(1)} copy-done((f32[3,32,32,128]{3,2,1,0:T(8,128)S(1)}, f32[3,32,32,128]{3,2,1,0:T(8,128)}, u32[]{:S(2)}) %copy-start) | copy-done | bytes 1572888
  2.0 0.0 copy-start.2
  2.0 0.7 copy-done.2
  2.8 46.8 %front.1 = (f32[32,32,128]{2,1,0:T(8,128)S(1)}, f32[128,8,128]{2,1,0:T(8,128)S(1)}) custom-call(f32[3,32,32,128]{3,2,1,0:T(8,128)S(1)} %copy-done, f32[6,8,128]{2,1,0:T(8,128)S(1)} %copy-done.2), custom_call_target="tpu_custom_call" | custom-call | tf_op jit(solution)/shard_map/front/pallas_call | solution.py:380
  49.5 0.0 copy-start.1
  49.6 1.1 %copy-done.1 = bf16[3,512,256]{2,1,0:T(8,128)(2,1)S(1)} copy-done((bf16[3,512,256]{2,1,0:T(8,128)(2,1)S(1)}, bf16[3,512,256]{2,1,0:T(8,128)(2,1)}, u32[]{:S(2)}) %copy-start.1) | copy-done | bytes 786456
  50.7 36.4 %spectral.1.modes_ref = f32[128,16,128]{2,1,0:T(8,128)S(1)} custom-call(f32[128,8,128]{2,1,0:T(8,128)S(1)} %get-tuple-element.5.tiles_ref, bf16[3,512,256]{2,1,0:T(8,128)(2,1)S(1)} %copy-done.1, bf16[3,4,1024,256]{3,2,1,0:T(8,128)(2,1)} %constant.8.clone.cycle_hbm), custom_call_target="tpu_custom_call" | custom-call | tf_op jit(solution)/shard_map/spectral/pallas_call | solution.py:596
  87.1 3.3 %solve.1 = f32[128,16,128]{2,1,0:T(8,128)} custom-call(f32[128,16,128]{2,1,0:T(8,128)S(1)} %spectral.1.modes_ref), custom_call_target="tpu_custom_call" | custom-call | tf_op jit(solution)/shard_map/solve/pallas_call | solution.py:676
  90.4 0.8 copy.7
Async XLA Ops:
  0.6 1.4 %copy-start = (f32[3,32,32,128]{3,2,1,0:T(8,128)S(1)}, f32[3,32,32,128]{3,2,1,0:T(8,128)}, u32[]{:S(2)}) copy-start(f32[3,32,32,128]{3,2,1,0:T(8,128)} %velocity.1) | copy-start | bytes 4718596
  2.0 0.7 copy-start.2
  49.5 1.1 %copy-start.1 = (bf16[3,512,256]{2,1,0:T(8,128)(2,1)S(1)}, bf16[3,512,256]{2,1,0:T(8,128)(2,1)}, u32[]{:S(2)}) copy-start(bf16[3,512,256]{2,1,0:T(8,128)(2,1)} %constant.7.clone.axial_hbm) | copy-start | bytes 2359300

commit v2 on v1

--- a/solution.py
+++ b/solution.py
@@ -80,13 +80,15 @@
     return {"theta": row, "gz": column}
 
 
-def exchange(velocity, flow, packed, landed, load_sem, send_sem, recv_sem, barrier):
+def exchange(velocity, flow, packed, landed, load_sem, send_sem, recv_sem, barrier, fetches):
     row, column = lax.axis_index("theta"), lax.axis_index("gz")
     below, above, left, right = neighbours(row, column)
     load = pltpu.make_async_copy(
         velocity, flow.at[:, pl.ds(3, LOCAL_T), pl.ds(Z_BASE, LOCAL_Z), :], load_sem
     )
     load.start()
+    for item in fetches:
+        item.start()
 
     def greet_row(i, carry):
         target = lax.rem(row + i, THETA_COUNT)
@@ -123,6 +125,7 @@
     for item in copies:
         item.start()
     load.wait()
+    fetches[0].wait()
     for side, first in ((0, Z_BASE + LOCAL_Z - 3), (1, Z_BASE)):
         for comp in range(3):
             for z in range(3):
@@ -173,7 +176,7 @@
             tensor[6, n, i] = tensor_magnitude(parts)
         return carry
 
-    lax.fori_loop(0, S_ROWS, strain_row, 0)
+    lax.fori_loop(0, S_ROWS, strain_row, 0, unroll=2)
 
 
 def filter_rows(flow, tensor, state, filtered):
@@ -283,7 +286,7 @@
         return carry
 
     lax.fori_loop(0, LOCAL_T, ratio_row, 0)
-    lax.fori_loop(0, S_ROWS, stress_row, 0)
+    lax.fori_loop(0, S_ROWS, stress_row, 0, unroll=2)
 
 
 def source_rows(flow, tensor, swirl, partial, source, radial):
@@ -332,82 +335,9 @@
             source[:, q * LOCAL_T + t, :] = value
         return carry
 
-    lax.fori_loop(1, S_ROWS - 1, swirl_row, 0)
-    lax.fori_loop(0, LOCAL_T, other_row, 0)
-    lax.fori_loop(0, LOCAL_T, join_row, 0)
-
-
-def front_kernel(
-    velocity,
-    radial,
-    ratio,
-    tiles,
-    flow,
-    packed,
-    landed,
-    tensor,
-    state,
-    filtered,
-    row_sums,
-    all_sums,
-    swirl,
-    partial,
-    source,
-    load_sem,
-    send_sem,
-    recv_sem,
-    sum_send_sem,
-    sum_recv_sem,
-):
-    barrier = pltpu.get_barrier_semaphore()
-    exchange(velocity, flow, packed, landed, load_sem, send_sem, recv_sem, barrier)
-    strain_rows(flow, tensor, radial)
-    numer, denom = filter_rows(flow, tensor, state, filtered)
-    numer, denom = sum_everywhere(numer, denom, row_sums, all_sums, sum_send_sem, sum_recv_sem)
-    width = radial[4][0:1]
-    numer = numer * (width * (2.0 / 256.0))
-    denom = denom * (width * width * (4.0 / 256.0))
-    coefficient = numer / (denom + epsilon_den)
-    eddy = jnp.broadcast_to(coefficient * width, (8, NR))
-    stress_rows(tensor, ratio, eddy)
-    source_rows(flow, tensor, swirl, partial, source, radial)
-    for s in range(8):
-        tiles[:, s, :] = source[s].T
-
-
-def front(velocity):
-    vmem = pl.BlockSpec(memory_space=pltpu.VMEM)
-    return pl.pallas_call(
-        front_kernel,
-        out_shape=(
-            jax.ShapeDtypeStruct((LOCAL_T, LOCAL_Z, NR), jnp.float32),
-            jax.ShapeDtypeStruct((NR, 8, 4 * LOCAL_T), jnp.float32),
-        ),
-        in_specs=[pl.BlockSpec(memory_space=pl.ANY), vmem],
-        out_specs=(vmem, vmem),
-        scratch_shapes=[
-            pltpu.VMEM((3, T_ROWS, Z_ROWS, NR), jnp.float32),
-            pltpu.VMEM((2, 9, LOCAL_T, NR), jnp.float32),
-            pltpu.VMEM((2, 9, LOCAL_T + 16, NR), jnp.float32),
-            pltpu.VMEM((7, S_ROWS, S_COLS, 8, NR), jnp.float32),
-            pltpu.VMEM((2, 21, Z_STEP, 8, NR), jnp.float32),
-            pltpu.VMEM((21, 2 * Z_STEP, 8, NR), jnp.float32),
-            pltpu.VMEM((THETA_COUNT, 8, NR), jnp.float32),
-            pltpu.VMEM((GZ_COUNT, 8, NR), jnp.float32),
-            pltpu.VMEM((LOCAL_T + 2, Z_STEP, 8, NR), jnp.float32),
-            pltpu.VMEM((LOCAL_T, Z_STEP, 8, NR), jnp.float32),
-            pltpu.VMEM((8, 4 * LOCAL_T, NR), jnp.float32),
-            pltpu.SemaphoreType.DMA,
-            pltpu.SemaphoreType.DMA((8,)),
-            pltpu.SemaphoreType.DMA((8,)),
-            pltpu.SemaphoreType.DMA((2,)),
-            pltpu.SemaphoreType.DMA((2,)),
-        ],
-        compiler_params=pltpu.CompilerParams(
-            collective_id=1, has_side_effects=True, vmem_limit_bytes=48 << 20
-        ),
-        name="front",
-    )(velocity, jnp.asarray(radial_table()))
+    lax.fori_loop(1, S_ROWS - 1, swirl_row, 0, unroll=2)
+    lax.fori_loop(0, LOCAL_T, other_row, 0, unroll=4)
+    lax.fori_loop(0, LOCAL_T, join_row, 0, unroll=2)
 
 
 def split_table(table):
@@ -455,48 +385,17 @@
     return total
 
 
-def meet_all(row, column, barrier, second):
-    def greet_row(i, carry):
-        pl.semaphore_signal(
-            barrier,
-            inc=1,
-            device_id={"theta": lax.rem(row + i, THETA_COUNT), "gz": column},
-            device_id_type=MESH_ID,
-        )
-        return carry
-
-    def greet_column(sem):
-        def greet(i, carry):
-            pl.semaphore_signal(
-                sem,
-                inc=1,
-                device_id={"theta": row, "gz": lax.rem(column + i, GZ_COUNT)},
-                device_id_type=MESH_ID,
-            )
-            return carry
-
-        return greet
-
-    lax.fori_loop(1, THETA_COUNT, greet_row, 0)
-    lax.fori_loop(1, GZ_COUNT, greet_column(barrier), 0)
-    pl.semaphore_wait(barrier, THETA_COUNT + GZ_COUNT - 2)
-    lax.fori_loop(1, GZ_COUNT, greet_column(second), 0)
-    pl.semaphore_wait(second, GZ_COUNT - 1)
-
-
-def spectral_kernel(
-    tiles_ref,
-    axial_hbm,
-    cycle_hbm,
-    modes_ref,
+def spectral_part(
+    tiles,
+    modes,
     planes,
     plane,
     axial,
     cycle,
     left,
     spectrum,
-    second,
-    table_sem,
+    fetch_axial,
+    fetch_cycle,
     send_sem,
     recv_sem,
     out_send_sem,
@@ -505,16 +404,11 @@
 ):
     row, column = lax.axis_index("theta"), lax.axis_index("gz")
     me = row * GZ_COUNT + column
-    fetch_axial = pltpu.make_async_copy(axial_hbm, axial, table_sem.at[0])
-    fetch_cycle = pltpu.make_async_copy(cycle_hbm, cycle, table_sem.at[1])
-    fetch_axial.start()
-    fetch_cycle.start()
-    meet_all(row, column, pltpu.get_barrier_semaphore(), second)
 
     def send_tile(i, carry):
         target = lax.rem(me + i, DEVICES)
         pltpu.make_async_remote_copy(
-            src_ref=tiles_ref.at[target],
+            src_ref=tiles.at[target],
             dst_ref=planes.at[me],
             send_sem=send_sem,
             recv_sem=recv_sem,
@@ -524,7 +418,7 @@
         return carry
 
     lax.fori_loop(1, DEVICES, send_tile, 0)
-    planes[me] = tiles_ref[me]
+    planes[me] = tiles[me]
     wait_bytes(planes.at[pl.ds(0, DEVICES - 1)], recv_sem)
     wait_bytes(planes.at[pl.ds(0, DEVICES - 1)], send_sem)
 
@@ -570,7 +464,7 @@
             def _():
                 pltpu.make_async_remote_copy(
                     src_ref=spectrum.at[target_column, rows],
-                    dst_ref=modes_ref.at[me],
+                    dst_ref=modes.at[me],
                     send_sem=out_send_sem,
                     recv_sem=out_recv_sem,
                     device_id={"theta": target_row, "gz": target_column},
@@ -584,43 +478,134 @@
 
     lax.fori_loop(0, GZ_COUNT // 2, transform, 0)
     own_rows = pl.ds(pl.multiple_of(row * LOCAL_K, LOCAL_K), LOCAL_K)
-    keep = pltpu.make_async_copy(spectrum.at[column, own_rows], modes_ref.at[me], own_sem)
+    keep = pltpu.make_async_copy(spectrum.at[column, own_rows], modes.at[me], own_sem)
     keep.start()
     keep.wait()
-    wait_bytes(modes_ref.at[pl.ds(0, DEVICES - 1)], out_send_sem)
-    wait_bytes(modes_ref.at[pl.ds(0, DEVICES - 1)], out_recv_sem)
-
-
-def spectral(tiles):
-    any_space = pl.BlockSpec(memory_space=pl.ANY)
+    wait_bytes(modes.at[pl.ds(0, DEVICES - 1)], out_send_sem)
+    wait_bytes(modes.at[pl.ds(0, DEVICES - 1)], out_recv_sem)
+
+
+def step_kernel(
+    velocity,
+    radial_hbm,
+    axial_hbm,
+    cycle_hbm,
+    ratio,
+    modes,
+    radial,
+    flow,
+    packed,
+    landed,
+    tensor,
+    state,
+    filtered,
+    row_sums,
+    all_sums,
+    swirl,
+    partial,
+    source,
+    tiles,
+    planes,
+    plane,
+    axial,
+    cycle,
+    left,
+    spectrum,
+    load_sem,
+    send_sem,
+    recv_sem,
+    sum_send_sem,
+    sum_recv_sem,
+    move_sem,
+):
+    fetches = [
+        pltpu.make_async_copy(source_ref, target, load_sem.at[n])
+        for n, (source_ref, target) in enumerate(
+            ((radial_hbm, radial), (axial_hbm, axial), (cycle_hbm, cycle)), 1
+        )
+    ]
+    barrier = pltpu.get_barrier_semaphore()
+    exchange(velocity, flow, packed, landed, load_sem.at[0], send_sem, recv_sem, barrier, fetches)
+    strain_rows(flow, tensor, radial)
+    numer, denom = filter_rows(flow, tensor, state, filtered)
+    numer, denom = sum_everywhere(numer, denom, row_sums, all_sums, sum_send_sem, sum_recv_sem)
+    width = radial[4][0:1]
+    numer = numer * (width * (2.0 / 256.0))
+    denom = denom * (width * width * (4.0 / 256.0))
+    coefficient = numer / (denom + epsilon_den)
+    eddy = jnp.broadcast_to(coefficient * width, (8, NR))
+    stress_rows(tensor, ratio, eddy)
+    source_rows(flow, tensor, swirl, partial, source, radial)
+    for s in range(8):
+        tiles[:, s, :] = source[s].T
+    spectral_part(
+        tiles,
+        modes,
+        planes,
+        plane,
+        axial,
+        cycle,
+        left,
+        spectrum,
+        fetches[1],
+        fetches[2],
+        *(move_sem.at[n] for n in range(5)),
+    )
+
+
+def step(velocity):
+    vmem = pl.BlockSpec(memory_space=pltpu.VMEM)
+    hbm = pl.BlockSpec(memory_space=pltpu.HBM)
     return pl.pallas_call(
-        spectral_kernel,
-        out_shape=jax.ShapeDtypeStruct((DEVICES, LOCAL_K, 128), jnp.float32),
-        in_specs=[pl.BlockSpec(memory_space=pltpu.VMEM), any_space, any_space],
-        out_specs=any_space,
+        step_kernel,
+        out_shape=(
+            jax.ShapeDtypeStruct((LOCAL_T, LOCAL_Z, NR), jnp.float32),
+            jax.ShapeDtypeStruct((DEVICES, LOCAL_K, 128), jnp.float32),
+        ),
+        in_specs=[hbm, hbm, hbm, hbm],
+        out_specs=(vmem, vmem),
         scratch_shapes=[
+            pltpu.VMEM((6, 8, NR), jnp.float32),
+            pltpu.VMEM((3, T_ROWS, Z_ROWS, NR), jnp.float32),
+            pltpu.VMEM((2, 9, LOCAL_T, NR), jnp.float32),
+            pltpu.VMEM((2, 9, LOCAL_T + 16, NR), jnp.float32),
+            pltpu.VMEM((7, S_ROWS, S_COLS, 8, NR), jnp.float32),
+            pltpu.VMEM((2, 21, Z_STEP, 8, NR), jnp.float32),
+            pltpu.VMEM((21, 2 * Z_STEP, 8, NR), jnp.float32),
+            pltpu.VMEM((THETA_COUNT, 8, NR), jnp.float32),
+            pltpu.VMEM((GZ_COUNT, 8, NR), jnp.float32),
+            pltpu.VMEM((LOCAL_T + 2, Z_STEP, 8, NR), jnp.float32),
+            pltpu.VMEM((LOCAL_T, Z_STEP, 8, NR), jnp.float32),
+            pltpu.VMEM((8, 4 * LOCAL_T, NR), jnp.float32),
+            pltpu.VMEM((NR, 8, 4 * LOCAL_T), jnp.float32),
             pltpu.VMEM((DEVICES, 8, 128), jnp.float32),
             pltpu.VMEM((NZ, NTH), jnp.float32),
             pltpu.VMEM((3, 2 * NZ, NZ), jnp.bfloat16),
             pltpu.VMEM((3, GZ_COUNT // 2, 2 * NTH, 4 * LOCAL_M), jnp.bfloat16),
             pltpu.VMEM((3, NZ, 2 * NTH), jnp.bfloat16),
             pltpu.VMEM((GZ_COUNT, NZ, 128), jnp.float32),
-            pltpu.SemaphoreType.REGULAR,
+            pltpu.SemaphoreType.DMA((4,)),
+            pltpu.SemaphoreType.DMA((8,)),
+            pltpu.SemaphoreType.DMA((8,)),
             pltpu.SemaphoreType.DMA((2,)),
-            pltpu.SemaphoreType.DMA,
-            pltpu.SemaphoreType.DMA,
-            pltpu.SemaphoreType.DMA,
-            pltpu.SemaphoreType.DMA,
-            pltpu.SemaphoreType.DMA,
+            pltpu.SemaphoreType.DMA((2,)),
+            pltpu.SemaphoreType.DMA((5,)),
         ],
         compiler_params=pltpu.CompilerParams(
             collective_id=0, has_side_effects=True, vmem_limit_bytes=48 << 20
         ),
-        name="spectral",
-    )(tiles, jnp.asarray(axial_table()), jnp.asarray(cycle_table()))
-
-
-def solve_kernel(modes_ref, out_ref, inverse, partial, pressure):
+        name="step",
+    )(
+        *(
+            pltpu.with_memory_space_constraint(jnp.asarray(value), pltpu.HBM)
+            for value in (velocity, radial_table(), axial_table(), cycle_table())
+        )
+    )
+
+
+def solve_kernel(modes_ref, ratio_ref, out_ref, ratio_out, inverse, partial, pressure, ratio_sem):
+    keep = pltpu.make_async_copy(ratio_ref, ratio_out, ratio_sem)
+    keep.start()
     row, column = lax.axis_index("theta"), lax.axis_index("gz")
     shape = (LOCAL_K, 128)
     theta_mode = column * LOCAL_M + lax.broadcasted_iota(jnp.int32, shape, 1) % LOCAL_M
@@ -669,25 +654,30 @@
         pressure[j] = high
     for k in range(LOCAL_K):
         out_ref[:, k, :] = pressure[:, k, :].T
-
-
-def solve(modes):
+    keep.wait()
+
+
+def solve(modes, ratio):
     vmem = pl.BlockSpec(memory_space=pltpu.VMEM)
-    out = pl.pallas_call(
+    anywhere = pl.BlockSpec(memory_space=pl.ANY)
+    pressure, ratio = pl.pallas_call(
         solve_kernel,
-        out_shape=jax.ShapeDtypeStruct((2 * LOCAL_M, LOCAL_K, NR), jnp.float32),
-        in_specs=[vmem],
-        out_specs=vmem,
-        scratch_shapes=[pltpu.VMEM((NR, LOCAL_K, 128), jnp.float32)] * 3,
+        out_shape=(
+            jax.ShapeDtypeStruct((2 * LOCAL_M, LOCAL_K, NR), jnp.float32),
+            jax.ShapeDtypeStruct((LOCAL_T, LOCAL_Z, NR), jnp.float32),
+        ),
+        in_specs=[vmem, anywhere],
+        out_specs=(vmem, pl.BlockSpec(memory_space=pltpu.HBM)),
+        scratch_shapes=[pltpu.VMEM((NR, LOCAL_K, 128), jnp.float32)] * 3 + [pltpu.SemaphoreType.DMA],
         compiler_params=pltpu.CompilerParams(vmem_limit_bytes=32 << 20),
         name="solve",
-    )(modes)
-    return out.reshape(2, LOCAL_M, LOCAL_K, NR)
+    )(modes, ratio)
+    return ratio, pressure.reshape(2, LOCAL_M, LOCAL_K, NR)
 
 
 def body(velocity):
-    ratio, tiles = front(velocity)
-    return (ratio, solve(spectral(tiles)))
+    ratio, modes = step(velocity)
+    return solve(modes, ratio)
 
 
 def solution(mesh):

time: 91.4 us -> 75 us (0.82)
  Pallas kernels: 86.5 us -> 74.3 us
  local copies, waits for them, and re-layouts: 4.06 us -> 0 us
    pallas_call x3 -> x2, Pallas kernels: 86.5 us -> 74.3 us  [the longest x1 70.9 us: step(): pl.pallas_call(step_kernel, out_shape=(jax.ShapeDtypeStruct((LOCAL_T, LOC...]
    unnamed x7 -> x0, local copies, waits for them, and re-layouts: 4.06 us -> none
where the time goes in v2:
time: 75 us; the launch traced here: 74.9 us
  Pallas kernels  74.3 us (99%)
    pallas_call x1, Pallas kernels, step(): pl.pallas_call(step_kernel, out_shape=(jax.ShapeDtypeStruct((LOCAL_T, LOC...  70.9 us
    pallas_call x1, Pallas kernels, solve(): pl.pallas_call(solve_kernel, out_shape=(jax.ShapeDtypeStruct((2 * LOCAL_M...  3.32 us

profile of v2, /device:TPU:1, one launch (start us, length us, event | category | flops | bytes accessed | tf_op | source)
XLA Modules:
  0.0 74.9 jit_solution(12737492515609776795)
XLA Ops:
  0.6 70.9 %step.1 = (f32[32,32,128]{2,1,0:T(8,128)S(1)}, f32[128,16,128]{2,1,0:T(8,128)S(1)}) custom-call(f32[3,32,32,128]{3,2,1,0:T(8,128)} %velocity.1, f32[6,8,128]{2,1,0:T(8,128)} %constant.6.clone.radial_hbm, bf16[3,512,256]{2,1,0:T(8,128)(2,1)} %constant.7.clone.axial_hbm, bf16[3,4,1024,256]{3,2,1,0:T(8,128)(2,1)} %constant.8.clone.cycle_hbm), custom_call_target="tpu_custom_call" | custom-call | tf_op jit(solution)/shard_map/step/pallas_call | solution.py:559
  71.6 3.3 %solve.1 = (f32[128,16,128]{2,1,0:T(8,128)}, f32[32,32,128]{2,1,0:T(8,128)}) custom-call(f32[128,16,128]{2,1,0:T(8,128)S(1)} %get-tuple-element.6.modes_ref, f32[32,32,128]{2,1,0:T(8,128)S(1)} %get-tuple-element.7.ratio_ref), custom_call_target="tpu_custom_call" | custom-call | tf_op jit(solution)/shard_map/solve/pallas_call | solution.py:663

commit v3 on v2

--- a/solution.py
+++ b/solution.py
@@ -80,35 +80,49 @@
     return {"theta": row, "gz": column}
 
 
-def exchange(velocity, flow, packed, landed, load_sem, send_sem, recv_sem, barrier, fetches):
+def exchange(velocity, flow, packed, landed, corners, load_sem, send_sem, recv_sem, fetches):
     row, column = lax.axis_index("theta"), lax.axis_index("gz")
     below, above, left, right = neighbours(row, column)
+    barrier = pltpu.get_barrier_semaphore()
+
+    def greet_row(i, carry):
+        target = lax.rem(row + i, THETA_COUNT)
+        pl.semaphore_signal(barrier, inc=1, device_id=device(target, column), device_id_type=MESH_ID)
+        return carry
+
+    def greet_column(i, carry):
+        target = lax.rem(column + i, GZ_COUNT)
+        pl.semaphore_signal(barrier, inc=1, device_id=device(row, target), device_id_type=MESH_ID)
+        return carry
+
     load = pltpu.make_async_copy(
         velocity, flow.at[:, pl.ds(3, LOCAL_T), pl.ds(Z_BASE, LOCAL_Z), :], load_sem
     )
     load.start()
-    for item in fetches:
-        item.start()
-
-    def greet_row(i, carry):
-        target = lax.rem(row + i, THETA_COUNT)
-        pl.semaphore_signal(barrier, inc=1, device_id=device(target, column), device_id_type=MESH_ID)
-        return carry
-
-    def greet_column(i, carry):
-        target = lax.rem(column + i, GZ_COUNT)
-        pl.semaphore_signal(barrier, inc=1, device_id=device(row, target), device_id_type=MESH_ID)
-        return carry
-
+    fetches[0].start()
     lax.fori_loop(1, THETA_COUNT, greet_row, 0)
     lax.fori_loop(1, GZ_COUNT, greet_column, 0)
     for r in (below, above):
         for c in (left, right):
             pl.semaphore_signal(barrier, inc=1, device_id=device(r, c), device_id_type=MESH_ID)
+    load.wait()
+    for side, first in ((0, Z_BASE + LOCAL_Z - 3), (1, Z_BASE)):
+        for comp in range(3):
+            for z in range(3):
+                packed[side, 3 * comp + z] = flow[comp, pl.ds(3, LOCAL_T), first + z, :]
+    sublane = lax.broadcasted_iota(jnp.int32, (8, NR), 0)
+    for side, near in ((0, 2), (1, 0)):
+        for comp in range(3):
+            for end, start, put, shift in ((0, LOCAL_T - 8, 5, 6), (1, 0, 2, 2)):
+                tile = packed[side, 3 * comp + near, pl.ds(start, 8), :]
+                other = packed[side, 3 * comp + 1, pl.ds(start, 8), :]
+                corners[0, 2 * side + end, comp] = jnp.where(
+                    sublane == put, pltpu.roll(other, shift, 0), tile
+                )
     pl.semaphore_wait(barrier, THETA_COUNT + GZ_COUNT + 2)
 
     def copy(n, source, target, r, c):
-        return pltpu.make_async_remote_copy(
+        item = pltpu.make_async_remote_copy(
             src_ref=source,
             dst_ref=target,
             send_sem=send_sem.at[n],
@@ -116,44 +130,54 @@
             device_id=device(r, c),
             device_id_type=MESH_ID,
         )
+        item.start()
+        return item
 
     inner = pl.ds(Z_BASE, LOCAL_Z)
-    copies = [
-        copy(0, velocity.at[:, pl.ds(LOCAL_T - 3, 3)], flow.at[:, pl.ds(0, 3), inner], above, column),
-        copy(1, velocity.at[:, pl.ds(0, 3)], flow.at[:, pl.ds(LOCAL_T + 3, 3), inner], below, column),
+    axial = [
+        copy(side, packed.at[side], landed.at[side], row, target)
+        for side, target in ((0, right), (1, left))
     ]
-    for item in copies:
-        item.start()
-    load.wait()
-    fetches[0].wait()
-    for side, first in ((0, Z_BASE + LOCAL_Z - 3), (1, Z_BASE)):
-        for comp in range(3):
-            for z in range(3):
-                packed[side, 3 * comp + z] = flow[comp, pl.ds(3, LOCAL_T), first + z, :]
+    rest = [
+        copy(2, velocity.at[:, pl.ds(LOCAL_T - 3, 3)], flow.at[:, pl.ds(0, 3), inner], above, column),
+        copy(3, velocity.at[:, pl.ds(0, 3)], flow.at[:, pl.ds(LOCAL_T + 3, 3), inner], below, column),
+    ]
     for side, target in ((0, right), (1, left)):
-        main, low, high = pl.ds(8, LOCAL_T), pl.ds(0, 8), pl.ds(LOCAL_T + 8, 8)
-        sides = [
-            copy(2 + 3 * side, packed.at[side], landed.at[side, :, main], row, target),
-            copy(3 + 3 * side, packed.at[side, :, pl.ds(LOCAL_T - 8, 8)], landed.at[side, :, low], above, target),
-            copy(4 + 3 * side, packed.at[side, :, pl.ds(0, 8)], landed.at[side, :, high], below, target),
-        ]
-        for item in sides:
-            item.start()
-        copies += sides
-    for item in copies:
-        item.wait()
-    for side, first in ((0, Z_BASE - 3), (1, Z_BASE + LOCAL_Z)):
-        for comp in range(3):
-            for z in range(3):
-                flow[comp, :, first + z, :] = landed[side, 3 * comp + z, pl.ds(5, T_ROWS), :]
+        for end, r in ((0, above), (1, below)):
+            n = 2 * side + end
+            rest.append(copy(4 + n, corners.at[0, n], corners.at[1, n], r, target))
+    fetches[1].start()
+    fetches[2].start()
+
+    def finish_axial():
+        for item in axial:
+            item.wait()
+        for side, first in ((0, Z_BASE - 3), (1, Z_BASE + LOCAL_Z)):
+            for comp in range(3):
+                for z in range(3):
+                    flow[comp, pl.ds(3, LOCAL_T), first + z, :] = landed[side, 3 * comp + z]
+
+    def finish_rest():
+        for item in rest:
+            item.wait()
+        for side, near, far in ((0, Z_BASE - 1, Z_BASE - 2), (1, Z_BASE + LOCAL_Z, Z_BASE + LOCAL_Z + 1)):
+            for comp in range(3):
+                low, high = corners.at[1, 2 * side, comp], corners.at[1, 2 * side + 1, comp]
+                for t, line, z in ((1, 6, near), (2, 7, near), (2, 5, far)):
+                    flow[comp, t, pl.ds(z, 1), :] = low[pl.ds(line, 1), :]
+                for t, line, z in ((0, 0, near), (1, 1, near), (0, 2, far)):
+                    flow[comp, LOCAL_T + 3 + t, pl.ds(z, 1), :] = high[pl.ds(line, 1), :]
+
+    return finish_axial, finish_rest
 
 
 def read_flow(flow, comp, t, q):
     return flow[comp, t, pl.ds(Z_BASE + q, 8, stride=Z_STEP), :]
 
 
-def strain_rows(flow, tensor, radial):
-    def strain_row(n, carry):
+def strain_rows(flow, tensor, radial, inner):
+    def strain_row(step, carry):
+        n = step + 3 if inner else step + (LOCAL_T - 2) * (step // 3)
         centre = [[read_flow(flow, c, n + 1, q) for q in range(-3, Z_STEP + 3)] for c in range(3)]
         for i in range(S_COLS):
             u = [centre[c][i + 1] for c in range(3)]
@@ -176,7 +200,7 @@
             tensor[6, n, i] = tensor_magnitude(parts)
         return carry
 
-    lax.fori_loop(0, S_ROWS, strain_row, 0, unroll=2)
+    lax.fori_loop(0, LOCAL_T - 2 if inner else 6, strain_row, 0, unroll=2)
 
 
 def filter_rows(flow, tensor, state, filtered):
@@ -364,7 +388,8 @@
     sine = (np.sin(angle) * scale).reshape(NTH, GZ_COUNT, LOCAL_M)
     upper = np.stack([cosine, -sine], axis=2)
     lower = np.stack([-sine, -cosine], axis=2)
-    both = np.concatenate([upper, lower], axis=0).reshape(2 * NTH, GZ_COUNT // 2, 4 * LOCAL_M)
+    both = np.concatenate([upper, lower], axis=0)[:, [0, 2, 1, 3, 4, 6, 5, 7]]
+    both = both.reshape(2 * NTH, GZ_COUNT // 2, 4 * LOCAL_M)
     return split_table(np.moveaxis(both, 1, 0))
 
 
@@ -450,14 +475,15 @@
     fetch_cycle.wait()
 
     def transform(step, carry):
-        pair = lax.rem(column // 2 + step, GZ_COUNT // 2)
-        both = product(left, cycle.at[:, pair])
-        spectrum[2 * pair] = both[:, :128]
-        spectrum[2 * pair + 1] = both[:, 128:]
+        chunk = lax.rem(2 * (column // 4) + lax.rem(column, 2) + step, GZ_COUNT // 2)
+        first = 4 * (chunk // 2) + lax.rem(chunk, 2)
+        both = product(left, cycle.at[:, chunk])
+        spectrum[first] = both[:, :128]
+        spectrum[first + 2] = both[:, 128:]
 
         def send_modes(i, inner):
-            target_column = 2 * pair + lax.rem(column + i // THETA_COUNT, 2)
-            target_row = lax.rem(row + i, THETA_COUNT)
+            target_column = first + 2 * lax.rem(i, 2)
+            target_row = lax.rem(row + i // 2, THETA_COUNT)
             rows = pl.ds(pl.multiple_of(target_row * LOCAL_K, LOCAL_K), LOCAL_K)
 
             @pl.when(jnp.logical_or(target_row != row, target_column != column))
@@ -492,10 +518,12 @@
     cycle_hbm,
     ratio,
     modes,
+    inverse,
     radial,
     flow,
     packed,
     landed,
+    corners,
     tensor,
     state,
     filtered,
@@ -524,9 +552,15 @@
             ((radial_hbm, radial), (axial_hbm, axial), (cycle_hbm, cycle)), 1
         )
     ]
-    barrier = pltpu.get_barrier_semaphore()
-    exchange(velocity, flow, packed, landed, load_sem.at[0], send_sem, recv_sem, barrier, fetches)
-    strain_rows(flow, tensor, radial)
+    finish_axial, finish_rest = exchange(
+        velocity, flow, packed, landed, corners, load_sem.at[0], send_sem, recv_sem, fetches
+    )
+    factor_rows(inverse)
+    fetches[0].wait()
+    finish_axial()
+    strain_rows(flow, tensor, radial, True)
+    finish_rest()
+    strain_rows(flow, tensor, radial, False)
     numer, denom = filter_rows(flow, tensor, state, filtered)
     numer, denom = sum_everywhere(numer, denom, row_sums, all_sums, sum_send_sem, sum_recv_sem)
     width = radial[4][0:1]
@@ -561,14 +595,16 @@
         out_shape=(
             jax.ShapeDtypeStruct((LOCAL_T, LOCAL_Z, NR), jnp.float32),
             jax.ShapeDtypeStruct((DEVICES, LOCAL_K, 128), jnp.float32),
+            jax.ShapeDtypeStruct((NR, LOCAL_K, 128), jnp.float32),
         ),
         in_specs=[hbm, hbm, hbm, hbm],
-        out_specs=(vmem, vmem),
+        out_specs=(vmem, vmem, vmem),
         scratch_shapes=[
             pltpu.VMEM((6, 8, NR), jnp.float32),
             pltpu.VMEM((3, T_ROWS, Z_ROWS, NR), jnp.float32),
             pltpu.VMEM((2, 9, LOCAL_T, NR), jnp.float32),
-            pltpu.VMEM((2, 9, LOCAL_T + 16, NR), jnp.float32),
+            pltpu.VMEM((2, 9, LOCAL_T, NR), jnp.float32),
+            pltpu.VMEM((2, 4, 3, 8, NR), jnp.float32),
             pltpu.VMEM((7, S_ROWS, S_COLS, 8, NR), jnp.float32),
             pltpu.VMEM((2, 21, Z_STEP, 8, NR), jnp.float32),
             pltpu.VMEM((21, 2 * Z_STEP, 8, NR), jnp.float32),
@@ -603,9 +639,7 @@
     )
 
 
-def solve_kernel(modes_ref, ratio_ref, out_ref, ratio_out, inverse, partial, pressure, ratio_sem):
-    keep = pltpu.make_async_copy(ratio_ref, ratio_out, ratio_sem)
-    keep.start()
+def diagonals():
     row, column = lax.axis_index("theta"), lax.axis_index("gz")
     shape = (LOCAL_K, 128)
     theta_mode = column * LOCAL_M + lax.broadcasted_iota(jnp.int32, shape, 1) % LOCAL_M
@@ -622,42 +656,57 @@
         extra = float(NR) if i == NR - 1 else 0.0
         return theta_sq * (1.0 / middle) + (axial_sq * middle + (2.0 * i + 1.0 + extra))
 
+    return diagonal
+
+
+def factor_rows(inverse):
+    diagonal = diagonals()
+    low, high = diagonal(0), diagonal(NR - 1)
+    for i in range(1, HALF):
+        j = NR - 1 - i
+        low_inverse, high_inverse = 1.0 / low, 1.0 / high
+        inverse[i - 1] = low_inverse
+        inverse[j + 1] = high_inverse
+        low = diagonal(i) - low_inverse * float(i * i)
+        high = diagonal(j) - high_inverse * float((j + 1) * (j + 1))
+    inverse[HALF - 1] = low
+    inverse[HALF] = high
+
+
+def solve_kernel(modes, inverse, ratio_ref, out_ref, ratio_out, partial, pressure, ratio_sem):
+    keep = pltpu.make_async_copy(ratio_ref, ratio_out, ratio_sem)
+    keep.start()
+
     def load(i):
-        return modes_ref[i] * (-(i + 0.5) / (NR * NR))
-
-    low_diag, low_value = diagonal(0), load(0)
-    high_diag, high_value = diagonal(NR - 1), load(NR - 1)
-    for step in range(1, HALF):
-        i = step
-        low_inverse = 1.0 / low_diag
-        inverse[i - 1] = low_inverse
-        partial[i - 1] = low_value
-        low_value = load(i) + (low_inverse * float(i)) * low_value
-        low_diag = diagonal(i) - low_inverse * float(i * i)
-        j = NR - 1 - step
-        high_inverse = 1.0 / high_diag
-        inverse[j + 1] = high_inverse
-        partial[j + 1] = high_value
-        high_value = load(j) + (high_inverse * float(j + 1)) * high_value
-        high_diag = diagonal(j) - high_inverse * float((j + 1) * (j + 1))
-    scale = 1.0 / (low_diag * high_diag - float(HALF * HALF))
-    low = (low_value * high_diag + float(HALF) * high_value) * scale
-    high = (high_value * low_diag + float(HALF) * low_value) * scale
+        return modes[i] * (-(i + 0.5) / (NR * NR))
+
+    low, high = load(0), load(NR - 1)
+    for i in range(1, HALF):
+        j = NR - 1 - i
+        partial[i - 1] = low
+        partial[j + 1] = high
+        low = load(i) + (inverse[i - 1] * float(i)) * low
+        high = load(j) + (inverse[j + 1] * float(j + 1)) * high
+    top, bottom = inverse[HALF - 1], inverse[HALF]
+    scale = 1.0 / (top * bottom - float(HALF * HALF))
+    low, high = (
+        (low * bottom + float(HALF) * high) * scale,
+        (high * top + float(HALF) * low) * scale,
+    )
     pressure[HALF - 1] = low
     pressure[HALF] = high
     for step in range(1, HALF):
-        i = HALF - 1 - step
+        i, j = HALF - 1 - step, HALF + step
         low = (partial[i] + float(i + 1) * low) * inverse[i]
+        high = (partial[j] + float(j) * high) * inverse[j]
         pressure[i] = low
-        j = HALF + step
-        high = (partial[j] + float(j) * high) * inverse[j]
         pressure[j] = high
     for k in range(LOCAL_K):
         out_ref[:, k, :] = pressure[:, k, :].T
     keep.wait()
 
 
-def solve(modes, ratio):
+def solve(modes, inverse, ratio):
     vmem = pl.BlockSpec(memory_space=pltpu.VMEM)
     anywhere = pl.BlockSpec(memory_space=pl.ANY)
     pressure, ratio = pl.pallas_call(
@@ -666,18 +715,18 @@
             jax.ShapeDtypeStruct((2 * LOCAL_M, LOCAL_K, NR), jnp.float32),
             jax.ShapeDtypeStruct((LOCAL_T, LOCAL_Z, NR), jnp.float32),
         ),
-        in_specs=[vmem, anywhere],
+        in_specs=[vmem, vmem, anywhere],
         out_specs=(vmem, pl.BlockSpec(memory_space=pltpu.HBM)),
-        scratch_shapes=[pltpu.VMEM((NR, LOCAL_K, 128), jnp.float32)] * 3 + [pltpu.SemaphoreType.DMA],
+        scratch_shapes=[pltpu.VMEM((NR, LOCAL_K, 128), jnp.float32)] * 2 + [pltpu.SemaphoreType.DMA],
         compiler_params=pltpu.CompilerParams(vmem_limit_bytes=32 << 20),
         name="solve",
-    )(modes, ratio)
+    )(modes, inverse, ratio)
     return ratio, pressure.reshape(2, LOCAL_M, LOCAL_K, NR)
 
 
 def body(velocity):
-    ratio, modes = step(velocity)
-    return solve(modes, ratio)
+    ratio, modes, inverse = step(velocity)
+    return solve(modes, inverse, ratio)
 
 
 def solution(mesh):

time: 75 us -> 68.4 us (0.912)
  Pallas kernels: 74.3 us -> 67.6 us
    pallas_call x1, Pallas kernels: 70.9 us -> 65 us  [step(): pl.pallas_call(step_kernel, out_shape=(jax.ShapeDtypeStruct((LOCAL_T, LOC...]
where the time goes in v3:
time: 68.4 us; the launch traced here: 68.2 us
  Pallas kernels  67.6 us (99%)
    pallas_call x1, Pallas kernels, step(): pl.pallas_call(step_kernel, out_shape=(jax.ShapeDtypeStruct((LOCAL_T, LOC...  65 us
    pallas_call x1, Pallas kernels, solve(): pl.pallas_call(solve_kernel, out_shape=(jax.ShapeDtypeStruct((2 * LOCAL_M...  2.66 us

profile of v3, /device:TPU:1, one launch (start us, length us, event | category | flops | bytes accessed | tf_op | source)
XLA Modules:
  0.0 68.2 jit_solution(7506444216496475784)
XLA Ops:
  0.6 65.0 %step.1 = (f32[32,32,128]{2,1,0:T(8,128)S(1)}, f32[128,16,128]{2,1,0:T(8,128)S(1)}, f32[128,16,128]{2,1,0:T(8,128)S(1)}) custom-call(f32[3,32,32,128]{3,2,1,0:T(8,128)} %velocity.1, f32[6,8,128]{2,1,0:T(8,128)} %constant.6.clone.radial_hbm, bf16[3,512,256]{2,1,0:T(8,128)(2,1)} %constant.7.clone.axial_hbm, bf16[3,4,1024,256]{3,2,1,0:T(8,128)(2,1)} %constant.8.clone.cycle_hbm), custom_call_target="tpu_custom_call" | custom-call | tf_op jit(solution)/shard_map/step/pallas_call | solution.py:593
  65.6 2.7 %solve.1 = (f32[128,16,128]{2,1,0:T(8,128)}, f32[32,32,128]{2,1,0:T(8,128)}) custom-call(f32[128,16,128]{2,1,0:T(8,128)S(1)} %get-tuple-element.7.modes, f32[128,16,128]{2,1,0:T(8,128)S(1)} %get-tuple-element.8.inverse, f32[32,32,128]{2,1,0:T(8,128)S(1)} %get-tuple-element.9.ratio_ref), custom_call_target="tpu_custom_call" | custom-call | tf_op jit(solution)/shard_map/solve/pallas_call | solution.py:712

commit v4 on v3

--- a/solution.py
+++ b/solution.py
@@ -56,8 +56,23 @@
     lower = upper.copy()
     upper[-1] = 0.0
     lower[0] = 0.0
-    rows = np.stack([1.0 / radius, DT / radius, upper, lower, width, radius])
-    return np.broadcast_to(rows[:, None, :], (6, 8, NR)).astype(np.float32)
+    rows = np.stack(
+        [
+            1.0 / radius,
+            DT / radius,
+            upper,
+            lower,
+            width,
+            radius,
+            upper / radius,
+            lower / radius,
+            time_step * radius,
+            2.0 * width,
+            (filter_ratio / 8.0) * width,
+            time_step * DT / radius,
+        ]
+    )
+    return np.broadcast_to(rows[:, None, :], (12, 8, NR)).astype(np.float32)
 
 
 def along_radius(field, radial):
@@ -195,15 +210,18 @@
                 0.5 * (dz[0] + dr[2]),
                 0.5 * (dt[2] + dz[1]),
             ]
+            size = tensor_magnitude(parts)
+            scale = size * radial[9]
+            tensor[6, n, i] = size
             for k in range(6):
                 tensor[k, n, i] = parts[k]
-            tensor[6, n, i] = tensor_magnitude(parts)
+                tensor[7 + k, n, i] = parts[k] * scale
         return carry
 
     lax.fori_loop(0, LOCAL_T - 2 if inner else 6, strain_row, 0, unroll=2)
 
 
-def filter_rows(flow, tensor, state, filtered):
+def filter_rows(flow, tensor, state, filtered, radial):
     span = range(-1, Z_STEP + 1)
 
     def across(n):
@@ -215,7 +233,7 @@
         for k in range(6):
             yield [tensor[k, n, q + 2] for q in span]
         for k in range(6):
-            yield [tensor[k, n, q + 2] * tensor[6, n, q + 2] for q in span]
+            yield [tensor[7 + k, n, q + 2] for q in span]
 
     def axial(values):
         pairs = [x + y for x, y in zip(values[:-1], values[1:])]
@@ -243,7 +261,7 @@
         for q in range(2 * Z_STEP):
             means = [filtered[c, q] for c in range(3)]
             smooth = [filtered[9 + k, q] for k in range(6)]
-            size = tensor_magnitude(smooth) * (filter_ratio / 16.0)
+            size = tensor_magnitude(smooth) * radial[10]
             lm, mm = [], []
             for k in range(6):
                 leonard = filtered[3 + k, q] - means[pair_first[k]] * means[pair_second[k]] * (1.0 / 16.0)
@@ -259,7 +277,7 @@
     return lax.fori_loop(0, LOCAL_T // 2, pair_rows, (zero, zero))
 
 
-def sum_everywhere(numer, denom, row_sums, all_sums, send_sem, recv_sem):
+def sum_everywhere(numer, denom, row_sums, all_sums, send_sem, recv_sem, meanwhile):
     row, column = lax.axis_index("theta"), lax.axis_index("gz")
     first = lax.broadcasted_iota(jnp.int32, (8, NR), 0) == 0
     tile = jnp.where(
@@ -281,6 +299,7 @@
             return carry
 
         lax.fori_loop(1, count, send, 0)
+        meanwhile[step]()
         others = buffer.at[pl.ds(0, count - 1)]
         wait_bytes(others, recv_sem.at[step])
         wait_bytes(others, send_sem.at[step])
@@ -294,74 +313,121 @@
     return tile[0:1], tile[1:2]
 
 
-def stress_rows(tensor, ratio, eddy):
-    def stress_row(n, carry):
-        for i in range(S_COLS):
-            viscosity = eddy * tensor[6, n, i]
-            scale = 2.0 * viscosity + 2.0 * nu_molecular
-            for k in range(6):
-                tensor[k, n, i] = tensor[k, n, i] * scale
-        return carry
-
-    def ratio_row(t, carry):
-        for q in range(Z_STEP):
-            value = eddy * tensor[6, t + 2, q + 2] * (1.0 / nu_molecular)
-            ratio[t, pl.ds(q, 8, stride=Z_STEP), :] = value
-        return carry
-
-    lax.fori_loop(0, LOCAL_T, ratio_row, 0)
-    lax.fori_loop(0, S_ROWS, stress_row, 0, unroll=2)
-
-
-def source_rows(flow, tensor, swirl, partial, source, radial):
+def force_parts(field, radial, cross):
+    still, moved = field
+    rest = along_radius(still, radial) + cross(0)
+    outer = pltpu.roll(moved, NR - 1, 1) * radial[2]
+    inner = pltpu.roll(moved, 1, 1) * radial[3]
+    return rest * (2.0 * nu_molecular * time_step), cross(7), outer, inner
+
+
+def swirl_rows(flow, tensor, swirl, radial):
     def swirl_row(n, carry):
         for q in range(Z_STEP):
             i = q + 2
-            shear = tensor[3, n, i]
-            force = (
-                along_radius(shear, radial)
-                + (tensor[1, n + 1, i] - tensor[1, n - 1, i]) * radial[1]
-                + (tensor[5, n, i + 1] - tensor[5, n, i - 1]) * DZ
-                + 2.0 * shear * radial[0]
-            )
-            swirl[n - 1, q] = read_flow(flow, 1, n + 1, q) + time_step * force
-        return carry
-
-    def other_row(t, carry):
+
+            def cross(k):
+                return (
+                    (tensor[k + 1, n + 1, i] - tensor[k + 1, n - 1, i]) * radial[1]
+                    + (tensor[k + 5, n, i + 1] - tensor[k + 5, n, i - 1]) * DZ
+                    + 2.0 * tensor[k + 3, n, i] * radial[0]
+                )
+
+            rest, here, outer, inner = force_parts((tensor[3, n, i], tensor[10, n, i]), radial, cross)
+            swirl[0, n - 1, q] = read_flow(flow, 1, n + 1, q) + rest
+            swirl[1, n - 1, q] = here
+            swirl[2, n - 1, q] = outer
+            swirl[3, n - 1, q] = inner
+        return carry
+
+    lax.fori_loop(1, S_ROWS - 1, swirl_row, 0, unroll=2)
+
+
+def form_rows(flow, tensor, form, radial, start, stop):
+    def form_row(t, carry):
         n = t + 2
         axial = []
         for q in range(-1, Z_STEP + 1):
             i = q + 2
-            shear = tensor[4, n, i]
-            force = (
-                along_radius(shear, radial)
-                + (tensor[5, n + 1, i] - tensor[5, n - 1, i]) * radial[1]
-                + (tensor[2, n, i + 1] - tensor[2, n, i - 1]) * DZ
-                + shear * radial[0]
-            )
-            axial.append(read_flow(flow, 2, n + 1, q) + time_step * force)
+
+            def cross(k):
+                return (
+                    (tensor[k + 5, n + 1, i] - tensor[k + 5, n - 1, i]) * radial[1]
+                    + (tensor[k + 2, n, i + 1] - tensor[k + 2, n, i - 1]) * DZ
+                    + tensor[k + 4, n, i] * radial[0]
+                )
+
+            rest, here, outer, inner = force_parts((tensor[4, n, i], tensor[11, n, i]), radial, cross)
+            axial.append((read_flow(flow, 2, n + 1, q) + rest, here, outer, inner))
         for q in range(Z_STEP):
             i = q + 2
-            normal = tensor[0, n, i]
-            force = (
-                along_radius(normal, radial)
-                + (tensor[3, n + 1, i] - tensor[3, n - 1, i]) * radial[1]
-                + (tensor[4, n, i + 1] - tensor[4, n, i - 1]) * DZ
-                + (normal - tensor[1, n, i]) * radial[0]
-            )
-            outward = (read_flow(flow, 0, n + 1, q) + time_step * force) * radial[5]
-            partial[t, q] = along_radius(outward, radial) * radial[0] + (axial[q + 2] - axial[q]) * DZ
-        return carry
-
+
+            def cross(k):
+                return (
+                    (tensor[k + 3, n + 1, i] - tensor[k + 3, n - 1, i]) * radial[1]
+                    + (tensor[k + 4, n, i + 1] - tensor[k + 4, n, i - 1]) * DZ
+                    + (tensor[k, n, i] - tensor[k + 1, n, i]) * radial[0]
+                )
+
+            rest, here, outer, inner = force_parts((tensor[0, n, i], tensor[7, n, i]), radial, cross)
+            rest = (read_flow(flow, 0, n + 1, q) + rest) * radial[5]
+            here, outer, inner = (value * radial[8] for value in (here, outer, inner))
+
+            def out(value):
+                return pltpu.roll(value, NR - 1, 1) * radial[6]
+
+            def back(value):
+                return pltpu.roll(value, 1, 1) * radial[7]
+
+            slope = [(high - low) * DZ for high, low in zip(axial[q + 2], axial[q])]
+            form[0, t, q] = slope[0] + (out(rest) - back(rest))
+            form[1, t, q] = slope[1] * time_step - (out(inner) + back(outer))
+            form[2, t, q] = slope[2] * time_step + out(here)
+            form[3, t, q] = slope[3] * time_step + back(here)
+            form[4, t, q] = out(outer)
+            form[5, t, q] = back(inner)
+        return carry
+
+    lax.fori_loop(start, stop, form_row, 0, unroll=2)
+
+
+def join_rows(swirl, form, radial):
     def join_row(t, carry):
+        for k in range(4):
+            for q in range(Z_STEP):
+                slope = (swirl[k, t + 2, q] - swirl[k, t, q]) * radial[11 if k else 1]
+                form[k, t, q] = form[k, t, q] + slope
+        return carry
+
+    lax.fori_loop(0, LOCAL_T, join_row, 0, unroll=2)
+
+
+def source_rows(form, source, coefficient):
+    here = jnp.broadcast_to(coefficient, (8, NR))
+    outer, inner = pltpu.roll(here, NR - 1, 1), pltpu.roll(here, 1, 1)
+    outer_two, inner_two = pltpu.roll(here, NR - 2, 1), pltpu.roll(here, 2, 1)
+
+    def source_row(t, carry):
         for q in range(Z_STEP):
-            value = partial[t, q] + (swirl[t + 2, q] - swirl[t, q]) * radial[1]
+            value = form[0, t, q] + here * form[1, t, q]
+            value = value + (outer * form[2, t, q] - inner * form[3, t, q])
+            value = value + (outer_two * form[4, t, q] + inner_two * form[5, t, q])
             source[:, q * LOCAL_T + t, :] = value
         return carry
 
-    lax.fori_loop(1, S_ROWS - 1, swirl_row, 0, unroll=2)
-    lax.fori_loop(0, LOCAL_T, other_row, 0, unroll=4)
-    lax.fori_loop(0, LOCAL_T, join_row, 0, unroll=2)
+    lax.fori_loop(0, LOCAL_T, source_row, 0, unroll=4)
+
+
+def ratio_rows(tensor, ratio, radial, coefficient):
+    scale = coefficient * (radial[4][0:1] * (1.0 / nu_molecular))
+    scale = jnp.broadcast_to(scale, (8, NR))
+
+    def ratio_row(t, carry):
+        for q in range(Z_STEP):
+            ratio[t, pl.ds(q, 8, stride=Z_STEP), :] = scale * tensor[6, t + 2, q + 2]
+        return carry
+
+    lax.fori_loop(0, LOCAL_T, ratio_row, 0, unroll=4)
 
 
 def split_table(table):
@@ -426,6 +492,7 @@
     out_send_sem,
     out_recv_sem,
     own_sem,
+    meanwhile,
 ):
     row, column = lax.axis_index("theta"), lax.axis_index("gz")
     me = row * GZ_COUNT + column
@@ -444,6 +511,7 @@
 
     lax.fori_loop(1, DEVICES, send_tile, 0)
     planes[me] = tiles[me]
+    meanwhile()
     wait_bytes(planes.at[pl.ds(0, DEVICES - 1)], recv_sem)
     wait_bytes(planes.at[pl.ds(0, DEVICES - 1)], send_sem)
 
@@ -530,7 +598,7 @@
     row_sums,
     all_sums,
     swirl,
-    partial,
+    form,
     source,
     tiles,
     planes,
@@ -561,15 +629,27 @@
     strain_rows(flow, tensor, radial, True)
     finish_rest()
     strain_rows(flow, tensor, radial, False)
-    numer, denom = filter_rows(flow, tensor, state, filtered)
-    numer, denom = sum_everywhere(numer, denom, row_sums, all_sums, sum_send_sem, sum_recv_sem)
-    width = radial[4][0:1]
-    numer = numer * (width * (2.0 / 256.0))
-    denom = denom * (width * width * (4.0 / 256.0))
-    coefficient = numer / (denom + epsilon_den)
-    eddy = jnp.broadcast_to(coefficient * width, (8, NR))
-    stress_rows(tensor, ratio, eddy)
-    source_rows(flow, tensor, swirl, partial, source, radial)
+    numer, denom = filter_rows(flow, tensor, state, filtered, radial)
+
+    def first_wait():
+        swirl_rows(flow, tensor, swirl, radial)
+        form_rows(flow, tensor, form, radial, 0, 10)
+
+    def second_wait():
+        form_rows(flow, tensor, form, radial, 10, LOCAL_T)
+        join_rows(swirl, form, radial)
+
+    numer, denom = sum_everywhere(
+        numer,
+        denom,
+        row_sums,
+        all_sums,
+        sum_send_sem,
+        sum_recv_sem,
+        (first_wait, second_wait),
+    )
+    coefficient = (numer * (1.0 / 256.0)) / (denom * (1.0 / 256.0) + epsilon_den)
+    source_rows(form, source, coefficient)
     for s in range(8):
         tiles[:, s, :] = source[s].T
     spectral_part(
@@ -584,6 +664,7 @@
         fetches[1],
         fetches[2],
         *(move_sem.at[n] for n in range(5)),
+        lambda: ratio_rows(tensor, ratio, radial, coefficient),
     )
 
 
@@ -600,18 +681,18 @@
         in_specs=[hbm, hbm, hbm, hbm],
         out_specs=(vmem, vmem, vmem),
         scratch_shapes=[
-            pltpu.VMEM((6, 8, NR), jnp.float32),
+            pltpu.VMEM((12, 8, NR), jnp.float32),
             pltpu.VMEM((3, T_ROWS, Z_ROWS, NR), jnp.float32),
             pltpu.VMEM((2, 9, LOCAL_T, NR), jnp.float32),
             pltpu.VMEM((2, 9, LOCAL_T, NR), jnp.float32),
             pltpu.VMEM((2, 4, 3, 8, NR), jnp.float32),
-            pltpu.VMEM((7, S_ROWS, S_COLS, 8, NR), jnp.float32),
+            pltpu.VMEM((13, S_ROWS, S_COLS, 8, NR), jnp.float32),
             pltpu.VMEM((2, 21, Z_STEP, 8, NR), jnp.float32),
             pltpu.VMEM((21, 2 * Z_STEP, 8, NR), jnp.float32),
             pltpu.VMEM((THETA_COUNT, 8, NR), jnp.float32),
             pltpu.VMEM((GZ_COUNT, 8, NR), jnp.float32),
-            pltpu.VMEM((LOCAL_T + 2, Z_STEP, 8, NR), jnp.float32),
-            pltpu.VMEM((LOCAL_T, Z_STEP, 8, NR), jnp.float32),
+            pltpu.VMEM((4, LOCAL_T + 2, Z_STEP, 8, NR), jnp.float32),
+            pltpu.VMEM((6, LOCAL_T, Z_STEP, 8, NR), jnp.float32),
             pltpu.VMEM((8, 4 * LOCAL_T, NR), jnp.float32),
             pltpu.VMEM((NR, 8, 4 * LOCAL_T), jnp.float32),
             pltpu.VMEM((DEVICES, 8, 128), jnp.float32),

time: 68.4 us -> 64.7 us (0.946)
  Pallas kernels: 67.6 us -> 63.9 us
    pallas_call x1, Pallas kernels: 65 us -> 61.3 us  [step(): pl.pallas_call(step_kernel, out_shape=(jax.ShapeDtypeStruct((LOCAL_T, LOC...]
where the time goes in v4:
time: 64.7 us; the launch traced here: 64.6 us
  Pallas kernels  63.9 us (99%)
    pallas_call x1, Pallas kernels, step(): pl.pallas_call(step_kernel, out_shape=(jax.ShapeDtypeStruct((LOCAL_T, LOC...  61.3 us
    pallas_call x1, Pallas kernels, solve(): pl.pallas_call(solve_kernel, out_shape=(jax.ShapeDtypeStruct((2 * LOCAL_M...  2.66 us

profile of v4, /device:TPU:1, one launch (start us, length us, event | category | flops | bytes accessed | tf_op | source)
XLA Modules:
  0.0 64.6 jit_solution(7166640244223048723)
XLA Ops:
  0.6 61.3 %step.1 = (f32[32,32,128]{2,1,0:T(8,128)S(1)}, f32[128,16,128]{2,1,0:T(8,128)S(1)}, f32[128,16,128]{2,1,0:T(8,128)S(1)}) custom-call(f32[3,32,32,128]{3,2,1,0:T(8,128)} %velocity.1, f32[12,8,128]{2,1,0:T(8,128)} %constant.6.clone.radial_hbm, bf16[3,512,256]{2,1,0:T(8,128)(2,1)} %constant.7.clone.axial_hbm, bf16[3,4,1024,256]{3,2,1,0:T(8,128)(2,1)} %constant.8.clone.cycle_hbm), custom_call_target="tpu_custom_call" | custom-call | tf_op jit(solution)/shard_map/step/pallas_call | solution.py:674
  61.9 2.7 %solve.1 = (f32[128,16,128]{2,1,0:T(8,128)}, f32[32,32,128]{2,1,0:T(8,128)}) custom-call(f32[128,16,128]{2,1,0:T(8,128)S(1)} %get-tuple-element.7.modes, f32[128,16,128]{2,1,0:T(8,128)S(1)} %get-tuple-element.8.inverse, f32[32,32,128]{2,1,0:T(8,128)S(1)} %get-tuple-element.9.ratio_ref), custom_call_target="tpu_custom_call" | custom-call | tf_op jit(solution)/shard_map/solve/pallas_call | solution.py:793

commit v5 on v4

--- a/solution.py
+++ b/solution.py
@@ -121,16 +121,16 @@
         for c in (left, right):
             pl.semaphore_signal(barrier, inc=1, device_id=device(r, c), device_id_type=MESH_ID)
     load.wait()
-    for side, first in ((0, Z_BASE + LOCAL_Z - 3), (1, Z_BASE)):
+    for side, first in ((0, Z_BASE + LOCAL_Z - 2), (1, Z_BASE)):
         for comp in range(3):
-            for z in range(3):
-                packed[side, 3 * comp + z] = flow[comp, pl.ds(3, LOCAL_T), first + z, :]
+            for z in range(2):
+                packed[side, 2 * comp + z] = flow[comp, pl.ds(3, LOCAL_T), first + z, :]
     sublane = lax.broadcasted_iota(jnp.int32, (8, NR), 0)
-    for side, near in ((0, 2), (1, 0)):
+    for side, near in ((0, 1), (1, 0)):
         for comp in range(3):
             for end, start, put, shift in ((0, LOCAL_T - 8, 5, 6), (1, 0, 2, 2)):
-                tile = packed[side, 3 * comp + near, pl.ds(start, 8), :]
-                other = packed[side, 3 * comp + 1, pl.ds(start, 8), :]
+                tile = packed[side, 2 * comp + near, pl.ds(start, 8), :]
+                other = packed[side, 2 * comp + 1 - near, pl.ds(start, 8), :]
                 corners[0, 2 * side + end, comp] = jnp.where(
                     sublane == put, pltpu.roll(other, shift, 0), tile
                 )
@@ -154,8 +154,8 @@
         for side, target in ((0, right), (1, left))
     ]
     rest = [
-        copy(2, velocity.at[:, pl.ds(LOCAL_T - 3, 3)], flow.at[:, pl.ds(0, 3), inner], above, column),
-        copy(3, velocity.at[:, pl.ds(0, 3)], flow.at[:, pl.ds(LOCAL_T + 3, 3), inner], below, column),
+        copy(2, velocity.at[:, pl.ds(LOCAL_T - 2, 2)], flow.at[:, pl.ds(1, 2), inner], above, column),
+        copy(3, velocity.at[:, pl.ds(0, 2)], flow.at[:, pl.ds(LOCAL_T + 3, 2), inner], below, column),
     ]
     for side, target in ((0, right), (1, left)):
         for end, r in ((0, above), (1, below)):
@@ -167,10 +167,10 @@
     def finish_axial():
         for item in axial:
             item.wait()
-        for side, first in ((0, Z_BASE - 3), (1, Z_BASE + LOCAL_Z)):
+        for side, first in ((0, Z_BASE - 2), (1, Z_BASE + LOCAL_Z)):
             for comp in range(3):
-                for z in range(3):
-                    flow[comp, pl.ds(3, LOCAL_T), first + z, :] = landed[side, 3 * comp + z]
+                for z in range(2):
+                    flow[comp, pl.ds(3, LOCAL_T), first + z, :] = landed[side, 2 * comp + z]
 
     def finish_rest():
         for item in rest:
@@ -192,11 +192,11 @@
 
 def strain_rows(flow, tensor, radial, inner):
     def strain_row(step, carry):
-        n = step + 3 if inner else step + (LOCAL_T - 2) * (step // 3)
-        centre = [[read_flow(flow, c, n + 1, q) for q in range(-3, Z_STEP + 3)] for c in range(3)]
-        for i in range(S_COLS):
-            u = [centre[c][i + 1] for c in range(3)]
-            dz = [(centre[c][i + 2] - centre[c][i]) * DZ for c in range(3)]
+        n = step + 3 if inner else step + 1 + (LOCAL_T - 2) * (step // 2)
+        centre = [[read_flow(flow, c, n + 1, q) for q in range(-2, Z_STEP + 2)] for c in range(3)]
+        for i in range(1, S_COLS - 1):
+            u = [centre[c][i] for c in range(3)]
+            dz = [(centre[c][i + 1] - centre[c][i - 1]) * DZ for c in range(3)]
             dt = [
                 (read_flow(flow, c, n + 2, i - 2) - read_flow(flow, c, n, i - 2)) * radial[1]
                 for c in range(3)
@@ -218,7 +218,7 @@
                 tensor[7 + k, n, i] = parts[k] * scale
         return carry
 
-    lax.fori_loop(0, LOCAL_T - 2 if inner else 6, strain_row, 0, unroll=2)
+    lax.fori_loop(0, LOCAL_T - 2 if inner else 4, strain_row, 0, unroll=2)
 
 
 def filter_rows(flow, tensor, state, filtered, radial):
@@ -321,44 +321,69 @@
     return rest * (2.0 * nu_molecular * time_step), cross(7), outer, inner
 
 
-def swirl_rows(flow, tensor, swirl, radial):
-    def swirl_row(n, carry):
+def face_rows(flow, tensor, swirl, drift, radial):
+    def face_row(t, carry):
+        n = t + 2
         for q in range(Z_STEP):
             i = q + 2
 
-            def cross(k):
+            def swirl_cross(k):
                 return (
                     (tensor[k + 1, n + 1, i] - tensor[k + 1, n - 1, i]) * radial[1]
                     + (tensor[k + 5, n, i + 1] - tensor[k + 5, n, i - 1]) * DZ
                     + 2.0 * tensor[k + 3, n, i] * radial[0]
                 )
 
-            rest, here, outer, inner = force_parts((tensor[3, n, i], tensor[10, n, i]), radial, cross)
-            swirl[0, n - 1, q] = read_flow(flow, 1, n + 1, q) + rest
-            swirl[1, n - 1, q] = here
-            swirl[2, n - 1, q] = outer
-            swirl[3, n - 1, q] = inner
-        return carry
-
-    lax.fori_loop(1, S_ROWS - 1, swirl_row, 0, unroll=2)
-
-
-def form_rows(flow, tensor, form, radial, start, stop):
-    def form_row(t, carry):
-        n = t + 2
-        axial = []
-        for q in range(-1, Z_STEP + 1):
-            i = q + 2
-
-            def cross(k):
+            def drift_cross(k):
                 return (
                     (tensor[k + 5, n + 1, i] - tensor[k + 5, n - 1, i]) * radial[1]
                     + (tensor[k + 2, n, i + 1] - tensor[k + 2, n, i - 1]) * DZ
                     + tensor[k + 4, n, i] * radial[0]
                 )
 
-            rest, here, outer, inner = force_parts((tensor[4, n, i], tensor[11, n, i]), radial, cross)
-            axial.append((read_flow(flow, 2, n + 1, q) + rest, here, outer, inner))
+            for comp, k, cross, target in ((1, 3, swirl_cross, swirl), (2, 4, drift_cross, drift)):
+                field = (tensor[k, n, i], tensor[k + 7, n, i])
+                rest, here, outer, inner = force_parts(field, radial, cross)
+                target[0, t + 1, q] = read_flow(flow, comp, n + 1, q) + rest
+                target[1, t + 1, q] = here
+                target[2, t + 1, q] = outer
+                target[3, t + 1, q] = inner
+        return carry
+
+    lax.fori_loop(0, LOCAL_T, face_row, 0, unroll=2)
+
+
+def send_faces(swirl, drift, edges, send_sem, recv_sem):
+    row, column = lax.axis_index("theta"), lax.axis_index("gz")
+    below, above, left, right = neighbours(row, column)
+    for k in range(4):
+        edges[0, 0, k] = drift[k, pl.ds(1, LOCAL_T), Z_STEP - 1, 7, :]
+        edges[0, 1, k] = drift[k, pl.ds(1, LOCAL_T), 0, 0, :]
+    copies = []
+    for n, (source, target, r, c) in enumerate(
+        (
+            (swirl.at[:, LOCAL_T], swirl.at[:, 0], above, column),
+            (swirl.at[:, 1], swirl.at[:, LOCAL_T + 1], below, column),
+            (edges.at[0, 0], edges.at[1, 0], row, right),
+            (edges.at[0, 1], edges.at[1, 1], row, left),
+        )
+    ):
+        item = pltpu.make_async_remote_copy(
+            src_ref=source,
+            dst_ref=target,
+            send_sem=send_sem.at[n],
+            recv_sem=recv_sem.at[n],
+            device_id=device(r, c),
+            device_id_type=MESH_ID,
+        )
+        item.start()
+        copies.append(item)
+    return copies
+
+
+def form_rows(flow, tensor, form, radial):
+    def form_row(t, carry):
+        n = t + 2
         for q in range(Z_STEP):
             i = q + 2
 
@@ -379,24 +404,32 @@
             def back(value):
                 return pltpu.roll(value, 1, 1) * radial[7]
 
-            slope = [(high - low) * DZ for high, low in zip(axial[q + 2], axial[q])]
-            form[0, t, q] = slope[0] + (out(rest) - back(rest))
-            form[1, t, q] = slope[1] * time_step - (out(inner) + back(outer))
-            form[2, t, q] = slope[2] * time_step + out(here)
-            form[3, t, q] = slope[3] * time_step + back(here)
+            form[0, t, q] = out(rest) - back(rest)
+            form[1, t, q] = -(out(inner) + back(outer))
+            form[2, t, q] = out(here)
+            form[3, t, q] = back(here)
             form[4, t, q] = out(outer)
             form[5, t, q] = back(inner)
         return carry
 
-    lax.fori_loop(start, stop, form_row, 0, unroll=2)
-
-
-def join_rows(swirl, form, radial):
+    lax.fori_loop(0, LOCAL_T, form_row, 0, unroll=2)
+
+
+def join_rows(swirl, drift, edges, form, radial):
+    sublane = lax.broadcasted_iota(jnp.int32, (8, NR), 0)
+
     def join_row(t, carry):
         for k in range(4):
+            inside = [drift[k, t + 1, q] for q in range(Z_STEP)]
+            low = jnp.broadcast_to(edges[1, 0, k, pl.ds(t, 1), :], (8, NR))
+            high = jnp.broadcast_to(edges[1, 1, k, pl.ds(t, 1), :], (8, NR))
+            low = jnp.where(sublane == 0, low, pltpu.roll(inside[-1], 1, 0))
+            high = jnp.where(sublane == 7, high, pltpu.roll(inside[0], 7, 0))
+            line = [low] + inside + [high]
             for q in range(Z_STEP):
-                slope = (swirl[k, t + 2, q] - swirl[k, t, q]) * radial[11 if k else 1]
-                form[k, t, q] = form[k, t, q] + slope
+                around = (swirl[k, t + 2, q] - swirl[k, t, q]) * radial[11 if k else 1]
+                along = (line[q + 2] - line[q]) * (DZ * time_step if k else DZ)
+                form[k, t, q] = form[k, t, q] + (around + along)
         return carry
 
     lax.fori_loop(0, LOCAL_T, join_row, 0, unroll=2)
@@ -598,6 +631,8 @@
     row_sums,
     all_sums,
     swirl,
+    drift,
+    edges,
     form,
     source,
     tiles,
@@ -612,6 +647,8 @@
     recv_sem,
     sum_send_sem,
     sum_recv_sem,
+    face_send_sem,
+    face_recv_sem,
     move_sem,
 ):
     fetches = [
@@ -631,13 +668,17 @@
     strain_rows(flow, tensor, radial, False)
     numer, denom = filter_rows(flow, tensor, state, filtered, radial)
 
+    faces = []
+
     def first_wait():
-        swirl_rows(flow, tensor, swirl, radial)
-        form_rows(flow, tensor, form, radial, 0, 10)
+        face_rows(flow, tensor, swirl, drift, radial)
+        faces.extend(send_faces(swirl, drift, edges, face_send_sem, face_recv_sem))
 
     def second_wait():
-        form_rows(flow, tensor, form, radial, 10, LOCAL_T)
-        join_rows(swirl, form, radial)
+        form_rows(flow, tensor, form, radial)
+        for item in faces:
+            item.wait()
+        join_rows(swirl, drift, edges, form, radial)
 
     numer, denom = sum_everywhere(
         numer,
@@ -683,8 +724,8 @@
         scratch_shapes=[
             pltpu.VMEM((12, 8, NR), jnp.float32),
             pltpu.VMEM((3, T_ROWS, Z_ROWS, NR), jnp.float32),
-            pltpu.VMEM((2, 9, LOCAL_T, NR), jnp.float32),
-            pltpu.VMEM((2, 9, LOCAL_T, NR), jnp.float32),
+            pltpu.VMEM((2, 6, LOCAL_T, NR), jnp.float32),
+            pltpu.VMEM((2, 6, LOCAL_T, NR), jnp.float32),
             pltpu.VMEM((2, 4, 3, 8, NR), jnp.float32),
             pltpu.VMEM((13, S_ROWS, S_COLS, 8, NR), jnp.float32),
             pltpu.VMEM((2, 21, Z_STEP, 8, NR), jnp.float32),
@@ -692,6 +733,8 @@
             pltpu.VMEM((THETA_COUNT, 8, NR), jnp.float32),
             pltpu.VMEM((GZ_COUNT, 8, NR), jnp.float32),
             pltpu.VMEM((4, LOCAL_T + 2, Z_STEP, 8, NR), jnp.float32),
+            pltpu.VMEM((4, LOCAL_T + 2, Z_STEP, 8, NR), jnp.float32),
+            pltpu.VMEM((2, 2, 4, LOCAL_T, NR), jnp.float32),
             pltpu.VMEM((6, LOCAL_T, Z_STEP, 8, NR), jnp.float32),
             pltpu.VMEM((8, 4 * LOCAL_T, NR), jnp.float32),
             pltpu.VMEM((NR, 8, 4 * LOCAL_T), jnp.float32),
@@ -706,6 +749,8 @@
             pltpu.SemaphoreType.DMA((8,)),
             pltpu.SemaphoreType.DMA((2,)),
             pltpu.SemaphoreType.DMA((2,)),
+            pltpu.SemaphoreType.DMA((4,)),
+            pltpu.SemaphoreType.DMA((4,)),
             pltpu.SemaphoreType.DMA((5,)),
         ],
         compiler_params=pltpu.CompilerParams(

time: 64.7 us -> 63.2 us (0.977)
  Pallas kernels: 63.9 us -> 62.4 us
    pallas_call x1, Pallas kernels: 61.3 us -> 59.8 us  [step(): pl.pallas_call(step_kernel, out_shape=(jax.ShapeDtypeStruct((LOCAL_T, LOC...]
where the time goes in v5:
time: 63.2 us; the launch traced here: 63.1 us
  Pallas kernels  62.4 us (99%)
  between operations  0.64 us (1%)
    pallas_call x1, Pallas kernels, step(): pl.pallas_call(step_kernel, out_shape=(jax.ShapeDtypeStruct((LOCAL_T, LOC...  59.8 us
    pallas_call x1, Pallas kernels, solve(): pl.pallas_call(solve_kernel, out_shape=(jax.ShapeDtypeStruct((2 * LOCAL_M...  2.66 us

profile of v5, /device:TPU:1, one launch (start us, length us, event | category | flops | bytes accessed | tf_op | source)
XLA Modules:
  0.0 63.1 jit_solution(4379484106332875441)
XLA Ops:
  0.6 59.8 %step.1 = (f32[32,32,128]{2,1,0:T(8,128)S(1)}, f32[128,16,128]{2,1,0:T(8,128)S(1)}, f32[128,16,128]{2,1,0:T(8,128)S(1)}) custom-call(f32[3,32,32,128]{3,2,1,0:T(8,128)} %velocity.1, f32[12,8,128]{2,1,0:T(8,128)} %constant.6.clone.radial_hbm, bf16[3,512,256]{2,1,0:T(8,128)(2,1)} %constant.7.clone.axial_hbm, bf16[3,4,1024,256]{3,2,1,0:T(8,128)(2,1)} %constant.8.clone.cycle_hbm), custom_call_target="tpu_custom_call" | custom-call | tf_op jit(solution)/shard_map/step/pallas_call | solution.py:715
  60.4 2.7 %solve.1 = (f32[128,16,128]{2,1,0:T(8,128)}, f32[32,32,128]{2,1,0:T(8,128)}) custom-call(f32[128,16,128]{2,1,0:T(8,128)S(1)} %get-tuple-element.7.modes, f32[128,16,128]{2,1,0:T(8,128)S(1)} %get-tuple-element.8.inverse, f32[32,32,128]{2,1,0:T(8,128)S(1)} %get-tuple-element.9.ratio_ref), custom_call_target="tpu_custom_call" | custom-call | tf_op jit(solution)/shard_map/solve/pallas_call | solution.py:838

commit v6 on v5

--- a/solution.py
+++ b/solution.py
@@ -56,6 +56,9 @@
     lower = upper.copy()
     upper[-1] = 0.0
     lower[0] = 0.0
+    out, back = upper / radius, lower / radius
+    outward, inward = time_step * radius * upper, time_step * radius * lower
+    centre = -(out * np.roll(inward, -1) + back * np.roll(outward, 1))
     rows = np.stack(
         [
             1.0 / radius,
@@ -64,15 +67,18 @@
             lower,
             width,
             radius,
-            upper / radius,
-            lower / radius,
+            out,
+            back,
             time_step * radius,
             2.0 * width,
             (filter_ratio / 8.0) * width,
             time_step * DT / radius,
+            out * np.roll(outward, -1),
+            centre,
+            back * np.roll(inward, 1),
         ]
     )
-    return np.broadcast_to(rows[:, None, :], (12, 8, NR)).astype(np.float32)
+    return np.broadcast_to(rows[:, None, :], (15, 8, NR)).astype(np.float32)
 
 
 def along_radius(field, radial):
@@ -153,16 +159,18 @@
         copy(side, packed.at[side], landed.at[side], row, target)
         for side, target in ((0, right), (1, left))
     ]
-    rest = [
-        copy(2, velocity.at[:, pl.ds(LOCAL_T - 2, 2)], flow.at[:, pl.ds(1, 2), inner], above, column),
-        copy(3, velocity.at[:, pl.ds(0, 2)], flow.at[:, pl.ds(LOCAL_T + 3, 2), inner], below, column),
-    ]
-    for side, target in ((0, right), (1, left)):
-        for end, r in ((0, above), (1, below)):
-            n = 2 * side + end
-            rest.append(copy(4 + n, corners.at[0, n], corners.at[1, n], r, target))
-    fetches[1].start()
-    fetches[2].start()
+    rest = []
+
+    def start_rest():
+        low, high = pl.ds(0, 2), pl.ds(LOCAL_T - 2, 2)
+        rest.append(copy(2, velocity.at[:, high], flow.at[:, pl.ds(1, 2), inner], above, column))
+        rest.append(copy(3, velocity.at[:, low], flow.at[:, pl.ds(LOCAL_T + 3, 2), inner], below, column))
+        for side, target in ((0, right), (1, left)):
+            for end, r in ((0, above), (1, below)):
+                n = 2 * side + end
+                rest.append(copy(4 + n, corners.at[0, n], corners.at[1, n], r, target))
+        fetches[1].start()
+        fetches[2].start()
 
     def finish_axial():
         for item in axial:
@@ -183,18 +191,19 @@
                 for t, line, z in ((0, 0, near), (1, 1, near), (0, 2, far)):
                     flow[comp, LOCAL_T + 3 + t, pl.ds(z, 1), :] = high[pl.ds(line, 1), :]
 
-    return finish_axial, finish_rest
+    return start_rest, finish_axial, finish_rest
 
 
 def read_flow(flow, comp, t, q):
     return flow[comp, t, pl.ds(Z_BASE + q, 8, stride=Z_STEP), :]
 
 
-def strain_rows(flow, tensor, radial, inner):
+def strain_rows(flow, tensor, radial, inner, columns):
     def strain_row(step, carry):
         n = step + 3 if inner else step + 1 + (LOCAL_T - 2) * (step // 2)
-        centre = [[read_flow(flow, c, n + 1, q) for q in range(-2, Z_STEP + 2)] for c in range(3)]
-        for i in range(1, S_COLS - 1):
+        needed = {i + d for i in columns for d in (-1, 0, 1)}
+        centre = [{i: read_flow(flow, c, n + 1, i - 2) for i in sorted(needed)} for c in range(3)]
+        for i in columns:
             u = [centre[c][i] for c in range(3)]
             dz = [(centre[c][i + 1] - centre[c][i - 1]) * DZ for c in range(3)]
             dt = [
@@ -313,12 +322,7 @@
     return tile[0:1], tile[1:2]
 
 
-def force_parts(field, radial, cross):
-    still, moved = field
-    rest = along_radius(still, radial) + cross(0)
-    outer = pltpu.roll(moved, NR - 1, 1) * radial[2]
-    inner = pltpu.roll(moved, 1, 1) * radial[3]
-    return rest * (2.0 * nu_molecular * time_step), cross(7), outer, inner
+still_scale = 2.0 * nu_molecular * time_step
 
 
 def face_rows(flow, tensor, swirl, drift, radial):
@@ -341,16 +345,19 @@
                     + tensor[k + 4, n, i] * radial[0]
                 )
 
+            size = tensor[6, n, i] * radial[9]
+            size_out, size_in = pltpu.roll(size, NR - 1, 1), pltpu.roll(size, 1, 1)
             for comp, k, cross, target in ((1, 3, swirl_cross, swirl), (2, 4, drift_cross, drift)):
-                field = (tensor[k, n, i], tensor[k + 7, n, i])
-                rest, here, outer, inner = force_parts(field, radial, cross)
-                target[0, t + 1, q] = read_flow(flow, comp, n + 1, q) + rest
-                target[1, t + 1, q] = here
-                target[2, t + 1, q] = outer
-                target[3, t + 1, q] = inner
-        return carry
-
-    lax.fori_loop(0, LOCAL_T, face_row, 0, unroll=2)
+                outer = pltpu.roll(tensor[k, n, i], NR - 1, 1) * radial[2]
+                inner = pltpu.roll(tensor[k, n, i], 1, 1) * radial[3]
+                rest = (outer - inner) + cross(0)
+                target[0, t + 1, q] = read_flow(flow, comp, n + 1, q) + rest * still_scale
+                target[1, t + 1, q] = cross(7)
+                target[2, t + 1, q] = size_out * outer
+                target[3, t + 1, q] = size_in * inner
+        return carry
+
+    lax.fori_loop(0, LOCAL_T, face_row, 0, unroll=4)
 
 
 def send_faces(swirl, drift, edges, send_sem, recv_sem):
@@ -394,25 +401,24 @@
                     + (tensor[k, n, i] - tensor[k + 1, n, i]) * radial[0]
                 )
 
-            rest, here, outer, inner = force_parts((tensor[0, n, i], tensor[7, n, i]), radial, cross)
-            rest = (read_flow(flow, 0, n + 1, q) + rest) * radial[5]
-            here, outer, inner = (value * radial[8] for value in (here, outer, inner))
-
-            def out(value):
-                return pltpu.roll(value, NR - 1, 1) * radial[6]
-
-            def back(value):
-                return pltpu.roll(value, 1, 1) * radial[7]
-
-            form[0, t, q] = out(rest) - back(rest)
-            form[1, t, q] = -(out(inner) + back(outer))
-            form[2, t, q] = out(here)
-            form[3, t, q] = back(here)
-            form[4, t, q] = out(outer)
-            form[5, t, q] = back(inner)
-        return carry
-
-    lax.fori_loop(0, LOCAL_T, form_row, 0, unroll=2)
+            still, moved = tensor[0, n, i], tensor[7, n, i]
+            rest = (read_flow(flow, 0, n + 1, q) + cross(0) * still_scale) * radial[5]
+            here = cross(7) * radial[8]
+            twice = (
+                pltpu.roll(still, NR - 2, 1) * radial[12]
+                + pltpu.roll(still, 2, 1) * radial[14]
+                + still * radial[13]
+            )
+            slope = pltpu.roll(rest, NR - 1, 1) * radial[6] - pltpu.roll(rest, 1, 1) * radial[7]
+            form[0, t, q] = slope + twice * (2.0 * nu_molecular)
+            form[1, t, q] = moved * radial[13]
+            form[2, t, q] = pltpu.roll(here, NR - 1, 1) * radial[6]
+            form[3, t, q] = pltpu.roll(here, 1, 1) * radial[7]
+            form[4, t, q] = pltpu.roll(moved, NR - 2, 1) * radial[12]
+            form[5, t, q] = pltpu.roll(moved, 2, 1) * radial[14]
+        return carry
+
+    lax.fori_loop(0, LOCAL_T, form_row, 0, unroll=4)
 
 
 def join_rows(swirl, drift, edges, form, radial):
@@ -432,7 +438,7 @@
                 form[k, t, q] = form[k, t, q] + (around + along)
         return carry
 
-    lax.fori_loop(0, LOCAL_T, join_row, 0, unroll=2)
+    lax.fori_loop(0, LOCAL_T, join_row, 0, unroll=4)
 
 
 def source_rows(form, source, coefficient):
@@ -657,15 +663,17 @@
             ((radial_hbm, radial), (axial_hbm, axial), (cycle_hbm, cycle)), 1
         )
     ]
-    finish_axial, finish_rest = exchange(
+    start_rest, finish_axial, finish_rest = exchange(
         velocity, flow, packed, landed, corners, load_sem.at[0], send_sem, recv_sem, fetches
     )
+    start_rest()
     factor_rows(inverse)
     fetches[0].wait()
+    strain_rows(flow, tensor, radial, True, (3, 4))
     finish_axial()
-    strain_rows(flow, tensor, radial, True)
+    strain_rows(flow, tensor, radial, True, (1, 2, 5, 6))
     finish_rest()
-    strain_rows(flow, tensor, radial, False)
+    strain_rows(flow, tensor, radial, False, range(1, S_COLS - 1))
     numer, denom = filter_rows(flow, tensor, state, filtered, radial)
 
     faces = []
@@ -722,7 +730,7 @@
         in_specs=[hbm, hbm, hbm, hbm],
         out_specs=(vmem, vmem, vmem),
         scratch_shapes=[
-            pltpu.VMEM((12, 8, NR), jnp.float32),
+            pltpu.VMEM((15, 8, NR), jnp.float32),
             pltpu.VMEM((3, T_ROWS, Z_ROWS, NR), jnp.float32),
             pltpu.VMEM((2, 6, LOCAL_T, NR), jnp.float32),
             pltpu.VMEM((2, 6, LOCAL_T, NR), jnp.float32),

time: 63.2 us -> 61.9 us (0.979)
  Pallas kernels: 62.4 us -> 61.2 us
    pallas_call x1, Pallas kernels: 59.8 us -> 58.5 us  [step(): pl.pallas_call(step_kernel, out_shape=(jax.ShapeDtypeStruct((LOCAL_T, LOC...]
where the time goes in v6:
time: 61.9 us; the launch traced here: 61.8 us
  Pallas kernels  61.2 us (99%)
  between operations  0.64 us (1%)
    pallas_call x1, Pallas kernels, step(): pl.pallas_call(step_kernel, out_shape=(jax.ShapeDtypeStruct((LOCAL_T, LOC...  58.5 us
    pallas_call x1, Pallas kernels, solve(): pl.pallas_call(solve_kernel, out_shape=(jax.ShapeDtypeStruct((2 * LOCAL_M...  2.66 us

profile of v6, /device:TPU:1, one launch (start us, length us, event | category | flops | bytes accessed | tf_op | source)
XLA Modules:
  0.0 61.8 jit_solution(4335824107802570913)
XLA Ops:
  0.6 58.5 %step.1 = (f32[32,32,128]{2,1,0:T(8,128)S(1)}, f32[128,16,128]{2,1,0:T(8,128)S(1)}, f32[128,16,128]{2,1,0:T(8,128)S(1)}) custom-call(f32[3,32,32,128]{3,2,1,0:T(8,128)} %velocity.1, f32[15,8,128]{2,1,0:T(8,128)} %constant.6.clone.radial_hbm, bf16[3,512,256]{2,1,0:T(8,128)(2,1)} %constant.7.clone.axial_hbm, bf16[3,4,1024,256]{3,2,1,0:T(8,128)(2,1)} %constant.8.clone.cycle_hbm), custom_call_target="tpu_custom_call" | custom-call | tf_op jit(solution)/shard_map/step/pallas_call | solution.py:723
  59.2 2.7 %solve.1 = (f32[128,16,128]{2,1,0:T(8,128)}, f32[32,32,128]{2,1,0:T(8,128)}) custom-call(f32[128,16,128]{2,1,0:T(8,128)S(1)} %get-tuple-element.7.modes, f32[128,16,128]{2,1,0:T(8,128)S(1)} %get-tuple-element.8.inverse, f32[32,32,128]{2,1,0:T(8,128)S(1)} %get-tuple-element.9.ratio_ref), custom_call_target="tpu_custom_call" | custom-call | tf_op jit(solution)/shard_map/solve/pallas_call | solution.py:846

commit v7 on v6

--- a/solution.py
+++ b/solution.py
@@ -807,7 +807,9 @@
     inverse[HALF] = high
 
 
-def solve_kernel(modes, inverse, ratio_ref, out_ref, ratio_out, partial, pressure, ratio_sem):
+def solve_kernel(
+    modes, inverse, ratio_ref, out_hbm, ratio_out, partial, pressure, turned, ratio_sem, out_sem
+):
     keep = pltpu.make_async_copy(ratio_ref, ratio_out, ratio_sem)
     keep.start()
 
@@ -835,9 +837,16 @@
         high = (partial[j] + float(j) * high) * inverse[j]
         pressure[i] = low
         pressure[j] = high
-    for k in range(LOCAL_K):
-        out_ref[:, k, :] = pressure[:, k, :].T
-    keep.wait()
+    copies = [keep]
+    for half in range(LOCAL_K // 8):
+        rows = pl.ds(8 * half, 8)
+        for k in range(8 * half, 8 * half + 8):
+            turned[:, k, :] = pressure[:, k, :].T
+        item = pltpu.make_async_copy(turned.at[:, rows], out_hbm.at[:, rows], out_sem.at[half])
+        item.start()
+        copies.append(item)
+    for item in copies:
+        item.wait()
 
 
 def solve(modes, inverse, ratio):
@@ -850,8 +859,13 @@
             jax.ShapeDtypeStruct((LOCAL_T, LOCAL_Z, NR), jnp.float32),
         ),
         in_specs=[vmem, vmem, anywhere],
-        out_specs=(vmem, pl.BlockSpec(memory_space=pltpu.HBM)),
-        scratch_shapes=[pltpu.VMEM((NR, LOCAL_K, 128), jnp.float32)] * 2 + [pltpu.SemaphoreType.DMA],
+        out_specs=(pl.BlockSpec(memory_space=pltpu.HBM), pl.BlockSpec(memory_space=pltpu.HBM)),
+        scratch_shapes=[pltpu.VMEM((NR, LOCAL_K, 128), jnp.float32)] * 2
+        + [
+            pltpu.VMEM((2 * LOCAL_M, LOCAL_K, NR), jnp.float32),
+            pltpu.SemaphoreType.DMA,
+            pltpu.SemaphoreType.DMA((LOCAL_K // 8,)),
+        ],
         compiler_params=pltpu.CompilerParams(vmem_limit_bytes=32 << 20),
         name="solve",
     )(modes, inverse, ratio)

time: 61.9 us -> 61.8 us (level)
  no operation moved by 1% of the time
where the time goes in v7:
time: 61.8 us; the launch traced here: 61.6 us
  Pallas kernels  61 us (99%)
  between operations  0.64 us (1%)
    pallas_call x1, Pallas kernels, step(): pl.pallas_call(step_kernel, out_shape=(jax.ShapeDtypeStruct((LOCAL_T, LOC...  58.5 us
    pallas_call x1, Pallas kernels, solve(): pl.pallas_call(solve_kernel, out_shape=(jax.ShapeDtypeStruct((2 * LOCAL_M...  2.5 us

profile of v7, /device:TPU:1, one launch (start us, length us, event | category | flops | bytes accessed | tf_op | source)
XLA Modules:
  0.0 61.6 jit_solution(5394353393381486318)
XLA Ops:
  0.6 58.5 %step.1 = (f32[32,32,128]{2,1,0:T(8,128)S(1)}, f32[128,16,128]{2,1,0:T(8,128)S(1)}, f32[128,16,128]{2,1,0:T(8,128)S(1)}) custom-call(f32[3,32,32,128]{3,2,1,0:T(8,128)} %velocity.1, f32[15,8,128]{2,1,0:T(8,128)} %constant.6.clone.radial_hbm, bf16[3,512,256]{2,1,0:T(8,128)(2,1)} %constant.7.clone.axial_hbm, bf16[3,4,1024,256]{3,2,1,0:T(8,128)(2,1)} %constant.8.clone.cycle_hbm), custom_call_target="tpu_custom_call" | custom-call | tf_op jit(solution)/shard_map/step/pallas_call | solution.py:723
  59.2 2.5 %solve.1 = (f32[128,16,128]{2,1,0:T(8,128)}, f32[32,32,128]{2,1,0:T(8,128)}) custom-call(f32[128,16,128]{2,1,0:T(8,128)S(1)} %get-tuple-element.7.modes, f32[128,16,128]{2,1,0:T(8,128)S(1)} %get-tuple-element.8.inverse, f32[32,32,128]{2,1,0:T(8,128)S(1)} %get-tuple-element.9.ratio_ref), custom_call_target="tpu_custom_call" | custom-call | tf_op jit(solution)/shard_map/solve/pallas_call | solution.py:855
